TPU v7x, 256 devices: a whole 4x4x8 slice. The times are simulated.
256 devices in a mesh: seq: 32 (over y, z), head: 8 (over x, core).
Axes of the slice: x: 4, y: 4, z: 8, core: 2. Of those that a mesh axis runs over, the one named last changes fastest.
Arguments:
- query_input: bfloat16 [16384, 2048], P(('seq', 'head')), may hold values from -6 to 6
- key_input: bfloat16 [16384, 2048], P(('seq', 'head')), may hold values from -40 to 40
- value_input: bfloat16 [16384, 4096], P(('seq', 'head')), may hold values from -40 to 40
- gate_input: bfloat16 [16384, 4096], P(('seq', 'head')), may hold values from -6 to 6
- write_strength: bfloat16 [16384, 32], P(('seq', 'head')), may hold values from 0.0009 to 0.91
- log_decay: bfloat16 [16384, 32], P(('seq', 'head')), may hold values from -0.81 to 0
- filter_query: bfloat16 [4, 2048], P(None, 'head'), may hold values from -3 to 3
- filter_key: bfloat16 [4, 2048], P(None, 'head'), may hold values from -3 to 3
- filter_value: bfloat16 [4, 4096], P(None, 'head'), may hold values from -3 to 3
- norm_gain: float32 [128], replicated, may hold values from 0.1 to 1.9
- out_weight: bfloat16 [4096, 2048], P('head'), may hold values from -0.09375 to 0.09375
Outputs:
- stratum_result: bfloat16 [16384, 2048], P(('seq', 'head'))
All inputs are finite; a program needn't handle non-finite values.
Results may differ from a plain program's by a relative error of at most 0.005.
Values may be sent and summed in bfloat16 or wider, within the bound.
A program may use at most 128 MiB of HBM per device.

v0:
```python
import jax
import jax.numpy as jnp
from jax import lax
from jax.sharding import PartitionSpec as P

HK = 16
HV = 32
DK = 128
DV = 128
CH = 64


exact_mode = lax.Precision.HIGHEST
norm_floor = 1e-06


def passed_along(value, axis, by):
    size = lax.axis_size(axis)
    pairs = [(i, i + by) for i in range(size) if 0 <= i + by < size]
    return lax.ppermute(value, axis, pairs)


def stretch_terms(query_rows, unit_keys, values, strength, forgetting_rates):
    block_width = forgetting_rates.shape[-1]
    value_width = values.shape[-1]
    key_width = unit_keys.shape[-1]
    token_index = lax.broadcasted_iota(jnp.int32, (block_width, block_width), 0)
    column_index = lax.broadcasted_iota(jnp.int32, (block_width, block_width), 1)
    inclusive = (column_index <= token_index).astype(jnp.float32)
    strict = (column_index < token_index).astype(jnp.float32)
    cumulative = jnp.cumsum(forgetting_rates, axis=-1)
    spread = cumulative[..., :, None] - cumulative[..., None, :]
    ratios = jnp.exp(spread * inclusive) * inclusive
    key_key = jnp.einsum("...id,...jd->...ij", unit_keys, unit_keys, precision=exact_mode)
    query_key = jnp.einsum("...id,...jd->...ij", query_rows, unit_keys, precision=exact_mode)
    lower_part = strength[..., :, None] * key_key * ratios * strict
    query_mix = query_key * ratios
    growth = jnp.exp(cumulative)
    right_side = jnp.concatenate(
        [strength[..., None] * values, (strength * growth)[..., None] * unit_keys], axis=-1
    )
    system = lower_part + jnp.eye(block_width, dtype=jnp.float32)
    solved = jax.scipy.linalg.solve_triangular(system, right_side, lower=True, unit_diagonal=True)
    written = solved[..., :value_width]
    erased = solved[..., value_width:]
    tail_decay = jnp.exp(cumulative[..., -1:] - cumulative)
    tailed = unit_keys * tail_decay[..., None]
    carry_map = jnp.exp(cumulative[..., -1])[..., None, None] * jnp.eye(
        key_width, dtype=jnp.float32
    ) - jnp.einsum("...id,...ie->...de", tailed, erased, precision=exact_mode)
    carry_add = jnp.einsum("...id,...ie->...de", tailed, written, precision=exact_mode)
    local_out = jnp.einsum("...ij,...je->...ie", query_mix, written, precision=exact_mode)
    entry_map = growth[..., None] * query_rows - jnp.einsum(
        "...ij,...jd->...id", query_mix, erased, precision=exact_mode
    )
    return (carry_map, carry_add, local_out, entry_map)


def causal_local(signal, before, filter_taps):
    length = signal.shape[0]
    padded = jnp.concatenate([before.astype(jnp.float32), signal.astype(jnp.float32)], axis=0)
    summed = jnp.zeros(signal.shape, jnp.float32)
    for offset in range(filter_taps.shape[0]):
        summed = summed + filter_taps[offset].astype(jnp.float32) * padded[offset : offset + length]
    return jax.nn.silu(summed)


def unit_rows(field):
    return field / jnp.sqrt(jnp.sum(field * field, axis=-1, keepdims=True) + norm_floor)


def to_blocks(per_token, blocks):
    token_count, head_count, inner_width = per_token.shape
    return per_token.reshape(blocks, token_count // blocks, head_count, inner_width).transpose(
        0, 2, 1, 3
    )


def apply_maps(maps, states):
    return jnp.einsum("hde,hef->hdf", maps, states, precision=exact_mode)


def gated_norm(core_out, gate_rows, norm_gain):
    token_count, head_count, head_width = core_out.shape
    inverse_rms = lax.rsqrt(jnp.mean(core_out * core_out, axis=-1, keepdims=True) + norm_floor)
    gating = jax.nn.silu(gate_rows.astype(jnp.float32)).reshape(token_count, head_count, head_width)
    return (
        (core_out * inverse_rms * norm_gain * gating)
        .astype(jnp.bfloat16)
        .reshape(token_count, head_count * head_width)
    )


def on_device(
    query_input,
    key_input,
    value_input,
    gate_input,
    write_strength,
    log_decay,
    filter_query,
    filter_key,
    filter_value,
    norm_gain,
    out_weight,
):
    grouped = (
        lax.all_to_all(query_input, "head", split_axis=1, concat_axis=0, tiled=True),
        lax.all_to_all(key_input, "head", split_axis=1, concat_axis=0, tiled=True),
        lax.all_to_all(value_input, "head", split_axis=1, concat_axis=0, tiled=True),
        lax.all_to_all(gate_input, "head", split_axis=1, concat_axis=0, tiled=True),
        lax.all_to_all(write_strength, "head", split_axis=1, concat_axis=0, tiled=True),
        lax.all_to_all(log_decay, "head", split_axis=1, concat_axis=0, tiled=True),
    )
    query_local, key_local, value_local, gate_local, strength_local, decay_local = grouped
    margin = filter_query.shape[0] - 1
    query_width = query_local.shape[1]
    key_width = key_local.shape[1]
    edge_rows = jnp.concatenate(
        [query_local[-margin:], key_local[-margin:], value_local[-margin:]], axis=1
    )
    before = passed_along(edge_rows, "seq", 1)
    query_rows = causal_local(query_local, before[:, :query_width], filter_query)
    unit_keys = causal_local(
        key_local, before[:, query_width : query_width + key_width], filter_key
    )
    values = causal_local(value_local, before[:, query_width + key_width :], filter_value)
    token_count = query_local.shape[0]
    key_heads = key_width // DK
    value_heads = value_local.shape[1] // DV
    sharing = HV // HK
    unit_keys = unit_rows(unit_keys.reshape(token_count, key_heads, DK))
    unit_keys = jnp.repeat(unit_keys, sharing, axis=1)
    query_rows = unit_rows(query_rows.reshape(token_count, key_heads, DK)) * DK ** (-0.5)
    query_rows = jnp.repeat(query_rows, sharing, axis=1)
    values = values.reshape(token_count, value_heads, DV)
    blocks = token_count // CH
    strength = (
        strength_local.astype(jnp.float32).reshape(blocks, CH, value_heads).transpose(0, 2, 1)
    )
    forgetting_rates = (
        decay_local.astype(jnp.float32).reshape(blocks, CH, value_heads).transpose(0, 2, 1)
    )
    carry_map, carry_add, local_out, entry_map = stretch_terms(
        to_blocks(query_rows, blocks),
        to_blocks(unit_keys, blocks),
        to_blocks(values, blocks),
        strength,
        forgetting_rates,
    )
    identity = jnp.broadcast_to(jnp.eye(DK, dtype=jnp.float32), (value_heads, DK, DK))
    zero_state = jnp.zeros((value_heads, DK, DV), jnp.float32)

    def compose(carried, pieces):
        product, offset = carried
        block_map, block_add = pieces
        return ((apply_maps(block_map, product), apply_maps(block_map, offset) + block_add), None)

    (span_map, span_add), unused = lax.scan(compose, (identity, zero_state), (carry_map, carry_add))

    def handoff_step(step_index, carried):
        arrived = passed_along(carried[1], "seq", 1)
        return (arrived, apply_maps(span_map, arrived) + span_add)

    entry_state, final_state = lax.fori_loop(
        0, lax.axis_size("seq") - 1, handoff_step, (zero_state, span_add)
    )

    def advance(running, pieces):
        block_map, block_add, block_out, block_entry = pieces
        emitted = block_out + jnp.einsum("hcd,hde->hce", block_entry, running, precision=exact_mode)
        return (apply_maps(block_map, running) + block_add, emitted)

    final_entry, core_out = lax.scan(
        advance, entry_state, (carry_map, carry_add, local_out, entry_map)
    )
    core_out = core_out.transpose(0, 2, 1, 3).reshape(token_count, value_heads, DV)
    normed = gated_norm(core_out, gate_local, norm_gain)
    projected = lax.psum_scatter(
        jnp.dot(normed, out_weight, preferred_element_type=jnp.float32),
        "head",
        scatter_dimension=0,
        tiled=True,
    )
    return projected.astype(jnp.bfloat16)


def solution(mesh):
    placed = (
        P(("seq", "head"), None),
        P(("seq", "head"), None),
        P(("seq", "head"), None),
        P(("seq", "head"), None),
        P(("seq", "head"), None),
        P(("seq", "head"), None),
        P(None, "head"),
        P(None, "head"),
        P(None, "head"),
        P(),
        P("head", None),
    )
    return jax.shard_map(
        on_device, mesh=mesh, in_specs=placed, out_specs=P(("seq", "head"), None), check_vma=False
    )
```

profile of v0, /device:TPU:121, one launch (start us, length us, event | category | flops | bytes accessed | tf_op | source)
XLA Modules:
  0.0 765.4 jit_solution(14248329500455291760)
XLA Ops:
  8.1 5.0 all-to-all-start
  21.2 4.8 all-to-all-start.4
  32.9 4.8 all-to-all-start.1
  38.7 5.5 all-to-all-done.1
  62.8 6.0 all-to-all-done.3
  68.8 5.0 all-to-all-start.5
  90.3 158.7 %custom-call.4 = f32[8,4,1,64,64]{3,4,2,1,0:T(8,128)} custom-call(f32[8,4,1,64,64]{4,3,2,1,0:T(8,128)} %fusion.28), custom_call_target="InvertDiagBlocksLowerTriangular" | custom-call | tf_op jit(solution)/shard_map/jit(_solve_triangular)/vmap(vmap())/triangular_solve | solution.py:43
  272.0 5.1 fusion.47
  277.2 5.5 multiply_subtract_fusion
  282.7 22.9 %while.39 = (s32[]{:T(128)}, f32[4,128,128]{2,1,0:T(8,128)S(1)}, f32[4,128,128]{2,1,0:T(8,128)S(1)}, f32[8,4,128,128]{3,2,1,0:T(8,128)}, f32[8,4,128,128]{3,2,1,0:T(8,128)}, /*index=5*/s32[]{:T(128)}, s32[]{:T(128)}) while((s32[]{:T(128)}, f32[4,128,128]{2,1,0:T(8,128)S(1)}, f32[4,128,128]{2,1,0:T(8,128)S(1)}, ...), condition=%wide.region_3.4_spmd.clone, body=%wide.region_2.3_spmd.clone.sunk | while | flops 201457664 | bytes 2885207 | solution.py:159
  305.6 322.9 %while.37 = (s32[]{:T(128)}, f32[4,128,128]{2,1,0:T(8,128)}, f32[4,128,128]{2,1,0:T(8,128)S(1)}, f32[4,128,128]{2,1,0:T(8,128)S(1)}, f32[4,128,128]{2,1,0:T(8,128)S(1)}, /*index=5*/s32[]{:T(128)}) while((s32[]{:T(128)}, f32[4,128,128]{2,1,0:T(8,128)}, f32[4,128,128]{2,1,0:T(8,128)S(1)}, f32[4,128,128]{2,1,0:T(8,128)S(1)}, ...), condition=%wide.region_5.6_spmd, body=%wide.region_4.5_spmd.sunk | while | flops 100728832 | bytes 3145865 | solution.py:165
  305.7 4.8 collective-permute-start
  315.9 5.3 collective-permute-start
  325.8 5.3 collective-permute-start
  335.1 5.0 collective-permute-start
  344.1 5.0 collective-permute-start
  353.1 5.0 collective-permute-start
  362.1 5.0 collective-permute-start
  371.5 5.0 collective-permute-start
  376.5 4.8 collective-permute-done
  382.0 5.0 collective-permute-start
  387.1 6.0 collective-permute-done
  393.7 5.1 collective-permute-start
  398.8 5.2 collective-permute-done
  404.8 5.3 collective-permute-start
  415.6 4.9 collective-permute-start
  420.5 7.5 collective-permute-done
  430.6 8.7 %collective-permute-done = f32[4,128,128]{2,1,0:T(8,128)S(1)} collective-permute-done((f32[4,128,128]{2,1,0:T(8,128)S(1)}, f32[4,128,128]{2,1,0:T(8,128)S(1)}, u32[]{:S(2)}, u32[]{:S(2)}) %collective-permute-start) | collective-permute-done | bytes 262176 | tf_op jit(solution)/shard_map/while/body/eval_jaxpr/ppermute | solution.py:20
  442.0 7.0 collective-permute-done
  451.8 6.0 collective-permute-done
  460.8 6.6 collective-permute-done
  470.0 7.3 collective-permute-done
  479.9 7.3 collective-permute-done
  489.9 7.4 collective-permute-done
  499.9 8.8 %collective-permute-done = f32[4,128,128]{2,1,0:T(8,128)S(1)} collective-permute-done((f32[4,128,128]{2,1,0:T(8,128)S(1)}, f32[4,128,128]{2,1,0:T(8,128)S(1)}, u32[]{:S(2)}, u32[]{:S(2)}) %collective-permute-start) | collective-permute-done | bytes 262176 | tf_op jit(solution)/shard_map/while/body/eval_jaxpr/ppermute | solution.py:20
  511.3 10.2 %collective-permute-done = f32[4,128,128]{2,1,0:T(8,128)S(1)} collective-permute-done((f32[4,128,128]{2,1,0:T(8,128)S(1)}, f32[4,128,128]{2,1,0:T(8,128)S(1)}, u32[]{:S(2)}, u32[]{:S(2)}) %collective-permute-start) | collective-permute-done | bytes 262176 | tf_op jit(solution)/shard_map/while/body/eval_jaxpr/ppermute | solution.py:20
  524.1 10.8 %collective-permute-done = f32[4,128,128]{2,1,0:T(8,128)S(1)} collective-permute-done((f32[4,128,128]{2,1,0:T(8,128)S(1)}, f32[4,128,128]{2,1,0:T(8,128)S(1)}, u32[]{:S(2)}, u32[]{:S(2)}) %collective-permute-start) | collective-permute-done | bytes 262176 | tf_op jit(solution)/shard_map/while/body/eval_jaxpr/ppermute | solution.py:20
  537.5 9.5 %collective-permute-done = f32[4,128,128]{2,1,0:T(8,128)S(1)} collective-permute-done((f32[4,128,128]{2,1,0:T(8,128)S(1)}, f32[4,128,128]{2,1,0:T(8,128)S(1)}, u32[]{:S(2)}, u32[]{:S(2)}) %collective-permute-start) | collective-permute-done | bytes 262176 | tf_op jit(solution)/shard_map/while/body/eval_jaxpr/ppermute | solution.py:20
  549.6 7.4 collective-permute-done
  559.9 6.2 collective-permute-done
  569.3 6.2 collective-permute-done
  578.4 6.7 collective-permute-done
  587.6 7.3 collective-permute-done
  597.6 7.3 collective-permute-done
  607.5 8.1 %collective-permute-done = f32[4,128,128]{2,1,0:T(8,128)S(1)} collective-permute-done((f32[4,128,128]{2,1,0:T(8,128)S(1)}, f32[4,128,128]{2,1,0:T(8,128)S(1)}, u32[]{:S(2)}, u32[]{:S(2)}) %collective-permute-start) | collective-permute-done | bytes 262176 | tf_op jit(solution)/shard_map/while/body/eval_jaxpr/ppermute | solution.py:20
  618.2 9.7 %collective-permute-done = f32[4,128,128]{2,1,0:T(8,128)S(1)} collective-permute-done((f32[4,128,128]{2,1,0:T(8,128)S(1)}, f32[4,128,128]{2,1,0:T(8,128)S(1)}, u32[]{:S(2)}, u32[]{:S(2)}) %collective-permute-start) | collective-permute-done | bytes 262176 | tf_op jit(solution)/shard_map/while/body/eval_jaxpr/ppermute | solution.py:20
  628.5 40.4 %while.38 = (s32[]{:T(128)}, f32[4,128,128]{2,1,0:T(8,128)}, f32[8,4,64,128]{3,2,1,0:T(8,128)}, f32[8,4,128,128]{3,2,1,0:T(8,128)}, f32[8,4,128,128]{3,2,1,0:T(8...) while((s32[]{:T(128)}, f32[4,128,128]{2,1,0:T(8,128)}, ...), condition=%wide.region_8.9_spmd, body=%wide.region_7.8_spmd.sunk | while | flops 151093248 | bytes 2230357 | solution.py:174
  678.1 78.7 %reduce-scatter.2.cloned.1.call-done = f32[64,2048]{1,0:T(8,128)} async-done(((f32[512,2048]{1,0:T(8,128)}), f32[64,2048]{1,0:T(8,128)}) %reduce-scatter.2.cloned.1.call-update) | async-done | bytes 524304 | tf_op jit(solution)/shard_map/reduce_scatter | solution.py:179
  (304 shorter events, 238.8 us)
Async XLA Ops:
  6.5 668.3 %copy-start = (bf16[512,2048]{1,0:T(8,128)(2,1)S(1)}, bf16[512,2048]{1,0:T(8,128)(2,1)}, u32[]{:S(2)}) copy-start(bf16[512,2048]{1,0:T(8,128)(2,1)} %param.27) | copy-start | bytes 6291460
  6.5 25.4 %copy-start.9 = (bf16[64,4096]{1,0:T(8,128)(2,1)S(1)}, bf16[64,4096]{1,0:T(8,128)(2,1)}, u32[]{:S(2)}) copy-start(bf16[64,4096]{1,0:T(8,128)(2,1)} %param.20) | copy-start | bytes 1572868
  8.1 13.2 %all-to-all-start = ((bf16[8,2,128]{2,1,0:T(2,128)(2,1)}), bf16[8,2,128]{2,1,0:T(2,128)(2,1)S(1)}, u32[]{:S(2)}, u32[]{:S(2)}) async-start(bf16[8,2,128]{2,1,0:T(2,128)(2,1)} %reshape.139), calls=%async_computation | async-start | bytes 8192 | tf_op jit(solution)/shard_map/all_to_all | solution.py:113
  21.2 11.6 %all-to-all-start.4 = ((bf16[8,2,128]{2,1,0:T(2,128)(2,1)}), bf16[8,2,128]{2,1,0:T(2,128)(2,1)S(1)}, u32[]{:S(2)}, u32[]{:S(2)}) async-start(bf16[8,2,128]{2,1,0:T(2,128)(2,1)} %reshape.141), calls=%async_computation.4 | async-start | bytes 8192 | tf_op jit(solution)/shard_map/all_to_all | solution.py:112
  32.9 11.3 %all-to-all-start.1 = ((bf16[64,8,256]{2,0,1:T(8,128)(2,1)}), bf16[64,8,256]{2,0,1:T(8,128)(2,1)S(1)}, u32[]{:S(2)}, u32[]{:S(2)}) async-start(bf16[64,8,256]{2,0,1:T(8,128)(2,1)} %bitcast.139), calls=%async_computation.1 | async-start | bytes 524288 | tf_op jit(solution)/shard_map/all_to_all | solution.py:108
  44.1 10.9 %copy-start.6 = (bf16[64,8,256]{2,0,1:T(8,128)(2,1)}, bf16[64,8,256]{2,0,1:T(8,128)(2,1)S(1)}, u32[]{:S(2)}) copy-start(bf16[64,8,256]{2,0,1:T(8,128)(2,1)S(1)} %all-to-all-done.1) | copy-start | bytes 786436
  44.1 10.8 %all-to-all-start.2 = ((bf16[64,8,256]{2,0,1:T(8,128)(2,1)}), bf16[64,8,256]{2,0,1:T(8,128)(2,1)S(1)}, u32[]{:S(2)}, u32[]{:S(2)}) async-start(bf16[64,8,256]{2,0,1:T(8,128)(2,1)} %bitcast.138), calls=%async_computation.2 | async-start | bytes 524288 | tf_op jit(solution)/shard_map/all_to_all | solution.py:109
  55.0 4.4 copy-start.7
  55.0 13.8 %all-to-all-start.3 = ((bf16[64,8,512]{2,0,1:T(8,128)(2,1)}), bf16[64,8,512]{2,0,1:T(8,128)(2,1)S(1)}, u32[]{:S(2)}, u32[]{:S(2)}) async-start(bf16[64,8,512]{2,0,1:T(8,128)(2,1)} %bitcast.137), calls=%async_computation.3 | async-start | bytes 1048576 | tf_op jit(solution)/shard_map/all_to_all | solution.py:110
  68.8 603.6 %all-to-all-start.5 = ((bf16[64,8,512]{2,0,1:T(8,128)(2,1)}), bf16[64,8,512]{2,0,1:T(8,128)(2,1)}, u32[]{:S(2)}, u32[]{:S(2)}) async-start(bf16[64,8,512]{2,0,1:T(8,128)(2,1)} %bitcast.136), calls=%async_computation.5 | async-start | bytes 1048576 | tf_op jit(solution)/shard_map/all_to_all | solution.py:111
  73.8 683.0 %reduce-scatter.2.cloned.1.call-start = ((), (), s32[]{:S(2)}) async-start(), calls=%async_computation.7 | async-start | bytes 4718592 | tf_op jit(solution)/shard_map/reduce_scatter | solution.py:179
  74.5 5.9 collective-permute-start.1
  248.9 2.2 copy-start.20
  248.9 2.2 copy-start.21
  249.0 2.2 copy-start.22
  272.0 5.1 copy-start.14
  305.7 9.6 %collective-permute-start = (f32[4,128,128]{2,1,0:T(8,128)S(1)}, f32[4,128,128]{2,1,0:T(8,128)S(1)}, u32[]{:S(2)}, u32[]{:S(2)}) collective-permute-start(f32[4,128,128]{2,1,0:T(8,128)S(1)} %get-tuple-element.307), channel_id=1, source_target_pairs={{0,8},{8,16},{16,24},{24,32},{32,40},{40,48},{48,56},{56,64},{64,7... | collective-permute-start | bytes 786440 | tf_op jit(solution)/shard_map/while/body/eval_jaxpr/ppermute | solution.py:20
  315.9 9.2 %collective-permute-start = (f32[4,128,128]{2,1,0:T(8,128)S(1)}, f32[4,128,128]{2,1,0:T(8,128)S(1)}, u32[]{:S(2)}, u32[]{:S(2)}) collective-permute-start(f32[4,128,128]{2,1,0:T(8,128)S(1)} %get-tuple-element.307), channel_id=1, source_target_pairs={{0,8},{8,16},{16,24},{24,32},{32,40},{40,48},{48,56},{56,64},{64,7... | collective-permute-start | bytes 786440 | tf_op jit(solution)/shard_map/while/body/eval_jaxpr/ppermute | solution.py:20
  325.8 8.6 %collective-permute-start = (f32[4,128,128]{2,1,0:T(8,128)S(1)}, f32[4,128,128]{2,1,0:T(8,128)S(1)}, u32[]{:S(2)}, u32[]{:S(2)}) collective-permute-start(f32[4,128,128]{2,1,0:T(8,128)S(1)} %get-tuple-element.307), channel_id=1, source_target_pairs={{0,8},{8,16},{16,24},{24,32},{32,40},{40,48},{48,56},{56,64},{64,7... | collective-permute-start | bytes 786440 | tf_op jit(solution)/shard_map/while/body/eval_jaxpr/ppermute | solution.py:20
  335.1 8.3 %collective-permute-start = (f32[4,128,128]{2,1,0:T(8,128)S(1)}, f32[4,128,128]{2,1,0:T(8,128)S(1)}, u32[]{:S(2)}, u32[]{:S(2)}) collective-permute-start(f32[4,128,128]{2,1,0:T(8,128)S(1)} %get-tuple-element.307), channel_id=1, source_target_pairs={{0,8},{8,16},{16,24},{24,32},{32,40},{40,48},{48,56},{56,64},{64,7... | collective-permute-start | bytes 786440 | tf_op jit(solution)/shard_map/while/body/eval_jaxpr/ppermute | solution.py:20
  344.1 8.3 %collective-permute-start = (f32[4,128,128]{2,1,0:T(8,128)S(1)}, f32[4,128,128]{2,1,0:T(8,128)S(1)}, u32[]{:S(2)}, u32[]{:S(2)}) collective-permute-start(f32[4,128,128]{2,1,0:T(8,128)S(1)} %get-tuple-element.307), channel_id=1, source_target_pairs={{0,8},{8,16},{16,24},{24,32},{32,40},{40,48},{48,56},{56,64},{64,7... | collective-permute-start | bytes 786440 | tf_op jit(solution)/shard_map/while/body/eval_jaxpr/ppermute | solution.py:20
  353.1 8.3 %collective-permute-start = (f32[4,128,128]{2,1,0:T(8,128)S(1)}, f32[4,128,128]{2,1,0:T(8,128)S(1)}, u32[]{:S(2)}, u32[]{:S(2)}) collective-permute-start(f32[4,128,128]{2,1,0:T(8,128)S(1)} %get-tuple-element.307), channel_id=1, source_target_pairs={{0,8},{8,16},{16,24},{24,32},{32,40},{40,48},{48,56},{56,64},{64,7... | collective-permute-start | bytes 786440 | tf_op jit(solution)/shard_map/while/body/eval_jaxpr/ppermute | solution.py:20
  362.1 8.7 %collective-permute-start = (f32[4,128,128]{2,1,0:T(8,128)S(1)}, f32[4,128,128]{2,1,0:T(8,128)S(1)}, u32[]{:S(2)}, u32[]{:S(2)}) collective-permute-start(f32[4,128,128]{2,1,0:T(8,128)S(1)} %get-tuple-element.307), channel_id=1, source_target_pairs={{0,8},{8,16},{16,24},{24,32},{32,40},{40,48},{48,56},{56,64},{64,7... | collective-permute-start | bytes 786440 | tf_op jit(solution)/shard_map/while/body/eval_jaxpr/ppermute | solution.py:20
  371.5 9.8 %collective-permute-start = (f32[4,128,128]{2,1,0:T(8,128)S(1)}, f32[4,128,128]{2,1,0:T(8,128)S(1)}, u32[]{:S(2)}, u32[]{:S(2)}) collective-permute-start(f32[4,128,128]{2,1,0:T(8,128)S(1)} %get-tuple-element.307), channel_id=1, source_target_pairs={{0,8},{8,16},{16,24},{24,32},{32,40},{40,48},{48,56},{56,64},{64,7... | collective-permute-start | bytes 786440 | tf_op jit(solution)/shard_map/while/body/eval_jaxpr/ppermute | solution.py:20
  382.0 11.0 %collective-permute-start = (f32[4,128,128]{2,1,0:T(8,128)S(1)}, f32[4,128,128]{2,1,0:T(8,128)S(1)}, u32[]{:S(2)}, u32[]{:S(2)}) collective-permute-start(f32[4,128,128]{2,1,0:T(8,128)S(1)} %get-tuple-element.307), channel_id=1, source_target_pairs={{0,8},{8,16},{16,24},{24,32},{32,40},{40,48},{48,56},{56,64},{64,7... | collective-permute-start | bytes 786440 | tf_op jit(solution)/shard_map/while/body/eval_jaxpr/ppermute | solution.py:20
  393.7 10.4 %collective-permute-start = (f32[4,128,128]{2,1,0:T(8,128)S(1)}, f32[4,128,128]{2,1,0:T(8,128)S(1)}, u32[]{:S(2)}, u32[]{:S(2)}) collective-permute-start(f32[4,128,128]{2,1,0:T(8,128)S(1)} %get-tuple-element.307), channel_id=1, source_target_pairs={{0,8},{8,16},{16,24},{24,32},{32,40},{40,48},{48,56},{56,64},{64,7... | collective-permute-start | bytes 786440 | tf_op jit(solution)/shard_map/while/body/eval_jaxpr/ppermute | solution.py:20
  404.8 10.1 %collective-permute-start = (f32[4,128,128]{2,1,0:T(8,128)S(1)}, f32[4,128,128]{2,1,0:T(8,128)S(1)}, u32[]{:S(2)}, u32[]{:S(2)}) collective-permute-start(f32[4,128,128]{2,1,0:T(8,128)S(1)} %get-tuple-element.307), channel_id=1, source_target_pairs={{0,8},{8,16},{16,24},{24,32},{32,40},{40,48},{48,56},{56,64},{64,7... | collective-permute-start | bytes 786440 | tf_op jit(solution)/shard_map/while/body/eval_jaxpr/ppermute | solution.py:20
  415.6 12.4 %collective-permute-start = (f32[4,128,128]{2,1,0:T(8,128)S(1)}, f32[4,128,128]{2,1,0:T(8,128)S(1)}, u32[]{:S(2)}, u32[]{:S(2)}) collective-permute-start(f32[4,128,128]{2,1,0:T(8,128)S(1)} %get-tuple-element.307), channel_id=1, source_target_pairs={{0,8},{8,16},{16,24},{24,32},{32,40},{40,48},{48,56},{56,64},{64,7... | collective-permute-start | bytes 786440 | tf_op jit(solution)/shard_map/while/body/eval_jaxpr/ppermute | solution.py:20
  428.7 10.6 %collective-permute-start = (f32[4,128,128]{2,1,0:T(8,128)S(1)}, f32[4,128,128]{2,1,0:T(8,128)S(1)}, u32[]{:S(2)}, u32[]{:S(2)}) collective-permute-start(f32[4,128,128]{2,1,0:T(8,128)S(1)} %get-tuple-element.307), channel_id=1, source_target_pairs={{0,8},{8,16},{16,24},{24,32},{32,40},{40,48},{48,56},{56,64},{64,7... | collective-permute-start | bytes 786440 | tf_op jit(solution)/shard_map/while/body/eval_jaxpr/ppermute | solution.py:20
  440.0 8.9 %collective-permute-start = (f32[4,128,128]{2,1,0:T(8,128)S(1)}, f32[4,128,128]{2,1,0:T(8,128)S(1)}, u32[]{:S(2)}, u32[]{:S(2)}) collective-permute-start(f32[4,128,128]{2,1,0:T(8,128)S(1)} %get-tuple-element.307), channel_id=1, source_target_pairs={{0,8},{8,16},{16,24},{24,32},{32,40},{40,48},{48,56},{56,64},{64,7... | collective-permute-start | bytes 786440 | tf_op jit(solution)/shard_map/while/body/eval_jaxpr/ppermute | solution.py:20
  449.6 8.1 %collective-permute-start = (f32[4,128,128]{2,1,0:T(8,128)S(1)}, f32[4,128,128]{2,1,0:T(8,128)S(1)}, u32[]{:S(2)}, u32[]{:S(2)}) collective-permute-start(f32[4,128,128]{2,1,0:T(8,128)S(1)} %get-tuple-element.307), channel_id=1, source_target_pairs={{0,8},{8,16},{16,24},{24,32},{32,40},{40,48},{48,56},{56,64},{64,7... | collective-permute-start | bytes 786440 | tf_op jit(solution)/shard_map/while/body/eval_jaxpr/ppermute | solution.py:20
  458.5 8.9 %collective-permute-start = (f32[4,128,128]{2,1,0:T(8,128)S(1)}, f32[4,128,128]{2,1,0:T(8,128)S(1)}, u32[]{:S(2)}, u32[]{:S(2)}) collective-permute-start(f32[4,128,128]{2,1,0:T(8,128)S(1)} %get-tuple-element.307), channel_id=1, source_target_pairs={{0,8},{8,16},{16,24},{24,32},{32,40},{40,48},{48,56},{56,64},{64,7... | collective-permute-start | bytes 786440 | tf_op jit(solution)/shard_map/while/body/eval_jaxpr/ppermute | solution.py:20
  468.1 9.2 %collective-permute-start = (f32[4,128,128]{2,1,0:T(8,128)S(1)}, f32[4,128,128]{2,1,0:T(8,128)S(1)}, u32[]{:S(2)}, u32[]{:S(2)}) collective-permute-start(f32[4,128,128]{2,1,0:T(8,128)S(1)} %get-tuple-element.307), channel_id=1, source_target_pairs={{0,8},{8,16},{16,24},{24,32},{32,40},{40,48},{48,56},{56,64},{64,7... | collective-permute-start | bytes 786440 | tf_op jit(solution)/shard_map/while/body/eval_jaxpr/ppermute | solution.py:20
  478.0 9.2 %collective-permute-start = (f32[4,128,128]{2,1,0:T(8,128)S(1)}, f32[4,128,128]{2,1,0:T(8,128)S(1)}, u32[]{:S(2)}, u32[]{:S(2)}) collective-permute-start(f32[4,128,128]{2,1,0:T(8,128)S(1)} %get-tuple-element.307), channel_id=1, source_target_pairs={{0,8},{8,16},{16,24},{24,32},{32,40},{40,48},{48,56},{56,64},{64,7... | collective-permute-start | bytes 786440 | tf_op jit(solution)/shard_map/while/body/eval_jaxpr/ppermute | solution.py:20
  487.9 9.3 %collective-permute-start = (f32[4,128,128]{2,1,0:T(8,128)S(1)}, f32[4,128,128]{2,1,0:T(8,128)S(1)}, u32[]{:S(2)}, u32[]{:S(2)}) collective-permute-start(f32[4,128,128]{2,1,0:T(8,128)S(1)} %get-tuple-element.307), channel_id=1, source_target_pairs={{0,8},{8,16},{16,24},{24,32},{32,40},{40,48},{48,56},{56,64},{64,7... | collective-permute-start | bytes 786440 | tf_op jit(solution)/shard_map/while/body/eval_jaxpr/ppermute | solution.py:20
  497.9 10.7 %collective-permute-start = (f32[4,128,128]{2,1,0:T(8,128)S(1)}, f32[4,128,128]{2,1,0:T(8,128)S(1)}, u32[]{:S(2)}, u32[]{:S(2)}) collective-permute-start(f32[4,128,128]{2,1,0:T(8,128)S(1)} %get-tuple-element.307), channel_id=1, source_target_pairs={{0,8},{8,16},{16,24},{24,32},{32,40},{40,48},{48,56},{56,64},{64,7... | collective-permute-start | bytes 786440 | tf_op jit(solution)/shard_map/while/body/eval_jaxpr/ppermute | solution.py:20
  509.4 12.1 %collective-permute-start = (f32[4,128,128]{2,1,0:T(8,128)S(1)}, f32[4,128,128]{2,1,0:T(8,128)S(1)}, u32[]{:S(2)}, u32[]{:S(2)}) collective-permute-start(f32[4,128,128]{2,1,0:T(8,128)S(1)} %get-tuple-element.307), channel_id=1, source_target_pairs={{0,8},{8,16},{16,24},{24,32},{32,40},{40,48},{48,56},{56,64},{64,7... | collective-permute-start | bytes 786440 | tf_op jit(solution)/shard_map/while/body/eval_jaxpr/ppermute | solution.py:20
  522.2 12.7 %collective-permute-start = (f32[4,128,128]{2,1,0:T(8,128)S(1)}, f32[4,128,128]{2,1,0:T(8,128)S(1)}, u32[]{:S(2)}, u32[]{:S(2)}) collective-permute-start(f32[4,128,128]{2,1,0:T(8,128)S(1)} %get-tuple-element.307), channel_id=1, source_target_pairs={{0,8},{8,16},{16,24},{24,32},{32,40},{40,48},{48,56},{56,64},{64,7... | collective-permute-start | bytes 786440 | tf_op jit(solution)/shard_map/while/body/eval_jaxpr/ppermute | solution.py:20
  535.6 11.4 %collective-permute-start = (f32[4,128,128]{2,1,0:T(8,128)S(1)}, f32[4,128,128]{2,1,0:T(8,128)S(1)}, u32[]{:S(2)}, u32[]{:S(2)}) collective-permute-start(f32[4,128,128]{2,1,0:T(8,128)S(1)} %get-tuple-element.307), channel_id=1, source_target_pairs={{0,8},{8,16},{16,24},{24,32},{32,40},{40,48},{48,56},{56,64},{64,7... | collective-permute-start | bytes 786440 | tf_op jit(solution)/shard_map/while/body/eval_jaxpr/ppermute | solution.py:20
  547.7 9.3 %collective-permute-start = (f32[4,128,128]{2,1,0:T(8,128)S(1)}, f32[4,128,128]{2,1,0:T(8,128)S(1)}, u32[]{:S(2)}, u32[]{:S(2)}) collective-permute-start(f32[4,128,128]{2,1,0:T(8,128)S(1)} %get-tuple-element.307), channel_id=1, source_target_pairs={{0,8},{8,16},{16,24},{24,32},{32,40},{40,48},{48,56},{56,64},{64,7... | collective-permute-start | bytes 786440 | tf_op jit(solution)/shard_map/while/body/eval_jaxpr/ppermute | solution.py:20
  557.8 8.4 %collective-permute-start = (f32[4,128,128]{2,1,0:T(8,128)S(1)}, f32[4,128,128]{2,1,0:T(8,128)S(1)}, u32[]{:S(2)}, u32[]{:S(2)}) collective-permute-start(f32[4,128,128]{2,1,0:T(8,128)S(1)} %get-tuple-element.307), channel_id=1, source_target_pairs={{0,8},{8,16},{16,24},{24,32},{32,40},{40,48},{48,56},{56,64},{64,7... | collective-permute-start | bytes 786440 | tf_op jit(solution)/shard_map/while/body/eval_jaxpr/ppermute | solution.py:20
  566.9 8.7 %collective-permute-start = (f32[4,128,128]{2,1,0:T(8,128)S(1)}, f32[4,128,128]{2,1,0:T(8,128)S(1)}, u32[]{:S(2)}, u32[]{:S(2)}) collective-permute-start(f32[4,128,128]{2,1,0:T(8,128)S(1)} %get-tuple-element.307), channel_id=1, source_target_pairs={{0,8},{8,16},{16,24},{24,32},{32,40},{40,48},{48,56},{56,64},{64,7... | collective-permute-start | bytes 786440 | tf_op jit(solution)/shard_map/while/body/eval_jaxpr/ppermute | solution.py:20
  576.2 8.8 %collective-permute-start = (f32[4,128,128]{2,1,0:T(8,128)S(1)}, f32[4,128,128]{2,1,0:T(8,128)S(1)}, u32[]{:S(2)}, u32[]{:S(2)}) collective-permute-start(f32[4,128,128]{2,1,0:T(8,128)S(1)} %get-tuple-element.307), channel_id=1, source_target_pairs={{0,8},{8,16},{16,24},{24,32},{32,40},{40,48},{48,56},{56,64},{64,7... | collective-permute-start | bytes 786440 | tf_op jit(solution)/shard_map/while/body/eval_jaxpr/ppermute | solution.py:20
  585.7 9.2 %collective-permute-start = (f32[4,128,128]{2,1,0:T(8,128)S(1)}, f32[4,128,128]{2,1,0:T(8,128)S(1)}, u32[]{:S(2)}, u32[]{:S(2)}) collective-permute-start(f32[4,128,128]{2,1,0:T(8,128)S(1)} %get-tuple-element.307), channel_id=1, source_target_pairs={{0,8},{8,16},{16,24},{24,32},{32,40},{40,48},{48,56},{56,64},{64,7... | collective-permute-start | bytes 786440 | tf_op jit(solution)/shard_map/while/body/eval_jaxpr/ppermute | solution.py:20
  595.6 9.2 %collective-permute-start = (f32[4,128,128]{2,1,0:T(8,128)S(1)}, f32[4,128,128]{2,1,0:T(8,128)S(1)}, u32[]{:S(2)}, u32[]{:S(2)}) collective-permute-start(f32[4,128,128]{2,1,0:T(8,128)S(1)} %get-tuple-element.307), channel_id=1, source_target_pairs={{0,8},{8,16},{16,24},{24,32},{32,40},{40,48},{48,56},{56,64},{64,7... | collective-permute-start | bytes 786440 | tf_op jit(solution)/shard_map/while/body/eval_jaxpr/ppermute | solution.py:20
  605.6 10.0 %collective-permute-start = (f32[4,128,128]{2,1,0:T(8,128)S(1)}, f32[4,128,128]{2,1,0:T(8,128)S(1)}, u32[]{:S(2)}, u32[]{:S(2)}) collective-permute-start(f32[4,128,128]{2,1,0:T(8,128)S(1)} %get-tuple-element.307), channel_id=1, source_target_pairs={{0,8},{8,16},{16,24},{24,32},{32,40},{40,48},{48,56},{56,64},{64,7... | collective-permute-start | bytes 786440 | tf_op jit(solution)/shard_map/while/body/eval_jaxpr/ppermute | solution.py:20
  616.2 11.6 %collective-permute-start = (f32[4,128,128]{2,1,0:T(8,128)S(1)}, f32[4,128,128]{2,1,0:T(8,128)S(1)}, u32[]{:S(2)}, u32[]{:S(2)}) collective-permute-start(f32[4,128,128]{2,1,0:T(8,128)S(1)} %get-tuple-element.307), channel_id=1, source_target_pairs={{0,8},{8,16},{16,24},{24,32},{32,40},{40,48},{48,56},{56,64},{64,7... | collective-permute-start | bytes 786440 | tf_op jit(solution)/shard_map/while/body/eval_jaxpr/ppermute | solution.py:20
  670.6 2.5 copy-start.18
  (44 other events, 41.0 us)
Sparse Core Ops, SparseCore 0:
  678.2 78.5 reduce-scatter.1
where the time goes:
time: 773 us; the launch traced here: 765 us
  waiting for transfers between devices  296 us (38%)
  other arithmetic  190 us (25%)
  starting transfers between devices  132 us (17%)
  matrix products  92.2 us (12%)
  local copies, waits for them, and re-layouts  40.2 us (5%)
  between operations  13.8 us (2%)
    ppermute x32, waiting for transfers between devices, passed_along(): return lax.ppermute(value, axis, pairs)  202 us
    another operation x4, other arithmetic, stretch_terms(): jax.scipy.linalg.solve_triangular(system, right_side, lower=True, unit_di...  160 us
    ppermute x32, starting transfers between devices, passed_along(): return lax.ppermute(value, axis, pairs)  103 us
    reduce_scatter x1, waiting for transfers between devices, on_device(): lax.psum_scatter(jnp.dot(normed, out_weight, preferred_element_type=jnp.f...  78.7 us
    dot_general x55, matrix products, apply_maps(): return jnp.einsum('hde,hef->hdf', maps, states, precision=exact_mode)  51.3 us
    while x86, local copies, waits for them, and re-layouts  17.3 us
    dot_general x8, matrix products, advance(): jnp.einsum('hcd,hde->hce', block_entry, running, precision=exact_mode)  15.8 us
  transfers between devices with their start and end apart: 39, of which 35 were waited for; matrix products, arithmetic and copies ran while one was open for 40% of the time, Pallas kernels for 0%

commit v1 on v0

v1 whole, which is shorter than its diff:
```python
import functools

import jax
import jax.numpy as jnp
from jax import lax
from jax.experimental import pallas as pl
from jax.experimental.pallas import tpu as pltpu
from jax.sharding import PartitionSpec as P

HK = 16
HV = 32
DK = 128
DV = 128
CH = 64
PAD = 16
NZ = 8
ROWS = 64
norm_floor = 1e-06
F32 = jnp.float32
BF16 = jnp.bfloat16
MESH = pl.DeviceIdType.MESH
VMEM_LIMIT = 60 * 1024 * 1024


def halves(x):
    high = x.astype(BF16)
    low = (x - high.astype(F32)).astype(BF16)
    return high, low


def dot(a, b, dims=((1,), (0,))):
    return lax.dot_general(a, b, (dims, ((), ())), preferred_element_type=F32)


def dot3(a, b, dims=((1,), (0,))):
    ah, al = a
    bh, bl = b
    return dot(ah, bh, dims) + (dot(ah, bl, dims) + dot(al, bh, dims))


def exchange_kernel(
    ns, nh, q, k, v, g, ws, ld, qo, ko, vo, go, wo, lo, send_sem, recv_sem, halo_send, halo_recv, own_sem
):
    seq = lax.axis_index("seq")
    me = lax.axis_index("head")
    rows = q.shape[0]
    ins = (q, k, v, g, ws, ld)
    outs = (qo, ko, vo, go, wo, lo)
    pads = (PAD, PAD, PAD, 0, 0, 0)
    last = jnp.logical_and(me == nh - 1, seq < ns - 1)
    barrier = pltpu.get_barrier_semaphore()
    for d in range(1, nh):
        pl.semaphore_signal(
            barrier, inc=1, device_id=(seq, lax.rem(me + d, nh)), device_id_type=MESH
        )

    @pl.when(seq > 0)
    def _():
        pl.semaphore_signal(barrier, inc=1, device_id=(seq - 1, nh - 1), device_id_type=MESH)

    @pl.when(last)
    def _():
        for d in range(nh):
            pl.semaphore_signal(barrier, inc=1, device_id=(seq + 1, d), device_id_type=MESH)

    def piece(ref, out, who):
        if out.shape[1] == ref.shape[1]:
            return ref
        width = out.shape[1]
        return ref.at[:, pl.ds(pl.multiple_of(who * width, width), width)]

    def own(a):
        return pltpu.make_async_copy(
            piece(ins[a], outs[a], me),
            outs[a].at[pl.ds(pl.multiple_of(pads[a] + me * rows, 16), rows), :],
            own_sem.at[a],
        )

    for a in range(6):
        own(a).start()
    pl.semaphore_wait(
        barrier, nh - 1 + jnp.where(seq > 0, 1, 0) + jnp.where(last, nh, 0)
    )

    def across(d, a, to, source):
        return pltpu.make_async_remote_copy(
            src_ref=piece(ins[a], outs[a], to),
            dst_ref=outs[a].at[pl.ds(pl.multiple_of(pads[a] + source * rows, 16), rows), :],
            send_sem=send_sem.at[d - 1, a],
            recv_sem=recv_sem.at[d - 1, a],
            device_id=(seq, to),
            device_id_type=MESH,
        )

    def halo(d, a):
        width = outs[a].shape[1]
        return pltpu.make_async_remote_copy(
            src_ref=ins[a].at[pl.ds(rows - PAD, PAD), pl.ds(d * width, width)],
            dst_ref=outs[a].at[pl.ds(0, PAD), :],
            send_sem=halo_send.at[d, a],
            recv_sem=halo_recv.at[a],
            device_id=(seq + 1, d),
            device_id_type=MESH,
        )

    order = [d for d in (4, 3, 5, 2, 6, 1, 7) if d < nh]
    for d in order:
        for a in range(6):
            across(d, a, lax.rem(me + d, nh), me).start()

    @pl.when(last)
    def _():
        for d in range(nh):
            for a in range(3):
                halo(d, a).start()

    for d in order:
        for a in range(6):
            across(d, a, lax.rem(me + d, nh), lax.rem(me + nh - d, nh)).wait()

    @pl.when(seq > 0)
    def _():
        for a in range(3):
            halo(0, a).wait_recv()

    @pl.when(last)
    def _():
        for d in range(nh):
            for a in range(3):
                halo(d, a).wait_send()

    for a in range(6):
        own(a).wait()


def exchange(ns, nh, arrays):
    rows = arrays[0].shape[0]
    total = rows * nh
    shapes = []
    for i, x in enumerate(arrays):
        width = x.shape[1] // nh if i < 4 else x.shape[1]
        shapes.append(jax.ShapeDtypeStruct((total + (PAD if i < 3 else 0), width), x.dtype))
    return pl.pallas_call(
        functools.partial(exchange_kernel, ns, nh),
        name="token_exchange",
        out_shape=shapes,
        in_specs=[pl.BlockSpec(memory_space=pl.ANY)] * 6,
        out_specs=[pl.BlockSpec(memory_space=pltpu.VMEM)] * 6,
        scratch_shapes=[
            pltpu.SemaphoreType.DMA((nh - 1, 6)),
            pltpu.SemaphoreType.DMA((nh - 1, 6)),
            pltpu.SemaphoreType.DMA((nh, 3)),
            pltpu.SemaphoreType.DMA((3,)),
            pltpu.SemaphoreType.DMA((6,)),
        ],
        compiler_params=pltpu.CompilerParams(
            collective_id=0, has_side_effects=True, vmem_limit_bytes=VMEM_LIMIT
        ),
    )(*arrays)


def local_kernel(
    where_ref, q_ref, k_ref, v_ref, ws_ref, ld_ref, fq_ref, fk_ref, fv_ref,
    chain_ref, qeff_ref, olocal_ref,
    key_s, query_s, w_s, e_s, mix_s, grow_s, tail_s, gamma_s, state_s,
):
    seq = where_ref[0]
    head = where_ref[1]
    tokens = ws_ref.shape[0]
    blocks = tokens // CH
    nheads = v_ref.shape[1] // DV
    nkeys = k_ref.shape[1] // DK
    share = nheads // nkeys
    row = lax.broadcasted_iota(jnp.int32, (CH, CH), 0)
    col = lax.broadcasted_iota(jnp.int32, (CH, CH), 1)
    incl = col <= row
    strict = col < row
    eye = (col == row).astype(F32)
    lower_ones = incl.astype(F32).astype(BF16)
    upper_ones = (row <= col).astype(F32).astype(BF16)
    allh = ws_ref.shape[1]
    pick = (
        lax.broadcasted_iota(jnp.int32, (allh, 128), 0)
        == head * nheads + lax.broadcasted_iota(jnp.int32, (allh, 128), 1)
    )
    pick = jnp.logical_and(pick, lax.broadcasted_iota(jnp.int32, (allh, 128), 1) < nheads)
    pick = pick.astype(F32).astype(BF16)
    pick_t = (
        lax.broadcasted_iota(jnp.int32, (8, allh), 1)
        == head * nheads + lax.broadcasted_iota(jnp.int32, (8, allh), 0)
    )
    pick_t = jnp.logical_and(pick_t, lax.broadcasted_iota(jnp.int32, (8, allh), 0) < nheads)
    pick_t = pick_t.astype(F32).astype(BF16)
    masks = []
    size = 1
    while size < CH:
        masks.append(
            jnp.logical_and(
                jnp.logical_and((row // size) % 2 == 1, (col // size) + 1 == row // size), strict
            )
        )
        size *= 2

    def filtered(ref, taps, start, lo, width):
        x = ref[pl.ds(start, CH + PAD), lo : lo + width].astype(F32)
        edge = lax.broadcasted_iota(jnp.int32, (CH + PAD, width), 0) < PAD
        x = jnp.where(jnp.logical_and(edge, jnp.logical_and(seq == 0, start == 0)), 0.0, x)
        total = None
        for j in range(4):
            term = taps[j : j + 1, lo : lo + width].astype(F32) * x[PAD - 3 + j : PAD - 3 + j + CH]
            total = term if total is None else total + term
        return total / (1.0 + jnp.exp(-total))

    def block_terms(c):
        start = pl.multiple_of(c * CH, CH)
        rows = pl.ds(start, CH)
        wsc = ws_ref[rows, :]
        ldc = ld_ref[rows, :]
        beta_c = dot(wsc, pick)
        dec_c = dot(ldc, pick)
        beta_r = dot(pick_t, wsc, ((1,), (1,)))
        dec_r = dot(pick_t, ldc, ((1,), (1,)))
        cum_c = dot(lower_ones, dec_c.astype(BF16))
        cum_r = dot(dec_r.astype(BF16), upper_ones)
        grow_c = jnp.exp(cum_c)
        grow_r = jnp.exp(cum_r)
        tail_c = jnp.exp(cum_c[CH - 1 : CH, :] - cum_c)
        gamma = grow_c[CH - 1 : CH, :]
        gamma_s[pl.ds(pl.multiple_of(c * 8, 8), 8), :] = jnp.broadcast_to(gamma, (8, 128))
        grow_s[rows, :] = grow_c
        tail_s[rows, :] = tail_c
        for p in range(nkeys):
            lanes = slice(p * DK, (p + 1) * DK)
            key = filtered(k_ref, fk_ref, start, p * DK, DK)
            key = key * lax.rsqrt(jnp.sum(key * key, axis=1, keepdims=True) + norm_floor)
            query = filtered(q_ref, fq_ref, start, p * DK, DK)
            query = query * (
                lax.rsqrt(jnp.sum(query * query, axis=1, keepdims=True) + norm_floor) * DK ** (-0.5)
            )
            key_s[rows, lanes] = key
            query_s[rows, lanes] = query
            kh, kl = halves(key)
            qh, ql = halves(query)
            kk = dot3((kh, kl), (kh, kl), ((1,), (1,)))
            qk = dot3((qh, ql), (kh, kl), ((1,), (1,)))
            for s in range(share):
                h = p * share + s
                spread = cum_c[:, h : h + 1] - cum_r[h : h + 1, :]
                ratios = jnp.where(incl, jnp.exp(jnp.where(incl, spread, 0.0)), 0.0)
                lower = jnp.where(strict, beta_c[:, h : h + 1] * kk * ratios, 0.0)
                mix_s[h, rows, :] = qk * ratios
                inv = eye - jnp.where(masks[0], lower, 0.0)
                for m in masks[1:]:
                    iv = halves(inv)
                    t = dot3(halves(jnp.where(m, lower, 0.0)), iv)
                    inv = inv - dot3(iv, halves(t))
                vals = filtered(v_ref, fv_ref, start, h * DV, DV)
                w_s[rows, h * DV : (h + 1) * DV] = dot3(
                    halves(inv * beta_r[h : h + 1, :]), halves(vals)
                )
                e_s[rows, h * DK : (h + 1) * DK] = dot3(
                    halves(inv * (beta_r[h : h + 1, :] * grow_r[h : h + 1, :])), (kh, kl)
                )

    def first(i, carry):
        block_terms(i)
        return carry

    lax.fori_loop(0, blocks, first, 0)

    eye_k = (
        lax.broadcasted_iota(jnp.int32, (DK, DK + DV), 0)
        == lax.broadcasted_iota(jnp.int32, (DK, DK + DV), 1)
    ).astype(F32)
    for h in range(nheads):
        state_s[h] = eye_k

    def second(c, carry):
        start = pl.multiple_of(c * CH, CH)
        rows = pl.ds(start, CH)
        grow_c = grow_s[rows, :]
        tail_c = tail_s[rows, :]
        gamma = gamma_s[pl.ds(pl.multiple_of(c * 8, 8), 8), :]
        for h in range(nheads):
            p = h // share
            key = key_s[rows, p * DK : (p + 1) * DK]
            query = query_s[rows, p * DK : (p + 1) * DK]
            state = state_s[h]
            e = e_s[rows, h * DK : (h + 1) * DK]
            w = w_s[rows, h * DV : (h + 1) * DV]
            left = jnp.concatenate([e, query * grow_c[:, h : h + 1]], axis=0)
            x = dot3(halves(left), halves(state))
            fresh = jnp.concatenate([-x[:CH, :DK], w - x[:CH, DK:]], axis=1)
            fr = halves(fresh)
            y = x[CH:] + dot3(halves(mix_s[h, rows, :]), fr)
            tailed = key * tail_c[:, h : h + 1]
            state_s[h] = gamma[0:1, h : h + 1] * state + dot3(
                halves(tailed), fr, ((0,), (0,))
            )
            qeff_ref[rows, h * DK : (h + 1) * DK] = y[:, :DK]
            olocal_ref[rows, h * DV : (h + 1) * DV] = y[:, DK:]
        return carry

    lax.fori_loop(0, blocks, second, 0)
    for h in range(nheads):
        for part in range(2):
            t = state_s[h, :, part * DK : (part + 1) * DK].T
            for r in range(DK // ROWS):
                chain_ref[h * 2 * (DK // ROWS) + part * (DK // ROWS) + r] = t[
                    r * ROWS : (r + 1) * ROWS
                ]


def local_terms(where, q, k, v, ws, ld, fq, fk, fv):
    tokens = ws.shape[0]
    nheads = v.shape[1] // DV
    nkeys = k.shape[1] // DK
    vm = pl.BlockSpec(memory_space=pltpu.VMEM)
    return pl.pallas_call(
        local_kernel,
        name="local_terms",
        out_shape=[
            jax.ShapeDtypeStruct((nheads * 2 * DK // ROWS, ROWS, DK), F32),
            jax.ShapeDtypeStruct((tokens, nheads * DK), F32),
            jax.ShapeDtypeStruct((tokens, nheads * DV), F32),
        ],
        in_specs=[pl.BlockSpec(memory_space=pltpu.SMEM)] + [vm] * 8,
        out_specs=[vm] * 3,
        scratch_shapes=[
            pltpu.VMEM((tokens, nkeys * DK), F32),
            pltpu.VMEM((tokens, nkeys * DK), F32),
            pltpu.VMEM((tokens, nheads * DV), F32),
            pltpu.VMEM((tokens, nheads * DK), F32),
            pltpu.VMEM((nheads, tokens, CH), F32),
            pltpu.VMEM((tokens, 128), F32),
            pltpu.VMEM((tokens, 128), F32),
            pltpu.VMEM((tokens // CH * 8, 128), F32),
            pltpu.VMEM((nheads, DK, DK + DV), F32),
        ],
        compiler_params=pltpu.CompilerParams(vmem_limit_bytes=VMEM_LIMIT),
    )(where, q, k, v, ws, ld, fq, fk, fv)


def chain_kernel(
    ns, nz, own_ref, entry_ref, before, here, map_h, map_l, earlier, later,
    pre_send, pre_recv, far_send, far_recv, relay_send, relay_two,
):
    seq = lax.axis_index("seq")
    head = lax.axis_index("head")
    ny = ns // nz
    z = lax.rem(seq, nz)
    y = seq // nz
    pieces = own_ref.shape[0]
    per_head = 2 * DK // ROWS
    half = per_head // 2
    nheads = pieces // per_head
    base = y * nz
    up = base + lax.rem(z + 1, nz)
    down = base + lax.rem(z + nz - 1, nz)
    mid = nz // 2
    is_end = z == nz - 1

    barrier = pltpu.get_barrier_semaphore()
    for other in (up, down):
        pl.semaphore_signal(barrier, inc=1, device_id=(other, head), device_id_type=MESH)

    @pl.when(jnp.logical_and(is_end, y > 0))
    def _():
        pl.semaphore_signal(barrier, inc=1, device_id=(seq - nz, head), device_id_type=MESH)

    @pl.when(jnp.logical_and(is_end, y < ny - 1))
    def _():
        pl.semaphore_signal(barrier, inc=1, device_id=(seq + nz, head), device_id_type=MESH)

    def split_maps(ref):
        for h in range(nheads):
            for r in range(half):
                hi, lo = halves(ref[h * per_head + r])
                map_h[h, r * ROWS : (r + 1) * ROWS, :] = hi
                map_l[h, r * ROWS : (r + 1) * ROWS, :] = lo

    split_maps(own_ref)
    pl.semaphore_wait(
        barrier,
        2
        + jnp.where(jnp.logical_and(is_end, y > 0), 1, 0)
        + jnp.where(jnp.logical_and(is_end, y < ny - 1), 1, 0),
    )

    def onward(n, source):
        return pltpu.make_async_remote_copy(
            src_ref=source.at[n],
            dst_ref=before.at[n],
            send_sem=pre_send.at[n],
            recv_sem=pre_recv.at[n],
            device_id=(up, head),
            device_id_type=MESH,
        )

    def to_group(m, source):
        return pltpu.make_async_remote_copy(
            src_ref=source.at[m],
            dst_ref=earlier.at[m],
            send_sem=far_send.at[m],
            recv_sem=far_recv.at[m],
            device_id=(seq + nz, head),
            device_id_type=MESH,
        )

    def relay(m, to, sem):
        return pltpu.make_async_remote_copy(
            src_ref=earlier.at[m],
            dst_ref=earlier.at[m],
            send_sem=sem.at[m],
            recv_sem=far_recv.at[m],
            device_id=(to, head),
            device_id_type=MESH,
        )

    def times_map(x, h):
        return dot3(halves(x), (map_h[h], map_l[h]))

    @pl.when(z == 0)
    def _():
        def send(n, c):
            onward(n, own_ref).start()
            return c

        lax.fori_loop(0, pieces, send, 0)

    @pl.when(z > 0)
    def _():
        def step(n, c):
            onward(n, here).wait_recv()
            h = n // per_head
            part = lax.rem(n, per_head)
            r = times_map(before[n], h)
            here[n] = r + jnp.where(part >= half, own_ref[n], 0.0)

            @pl.when(z < nz - 1)
            def _():
                onward(n, here).start()

            return c

        lax.fori_loop(0, pieces, step, 0)

    npe = nheads * half

    @pl.when(is_end)
    def _():
        @pl.when(y == 0)
        def _():
            def send(m, c):
                h = m // half
                r = lax.rem(m, half)
                later[m] = here[h * per_head + half + r]
                to_group(m, later).start()
                return c

            lax.fori_loop(0, npe, send, 0)

        @pl.when(y > 0)
        def _():
            split_maps(here)

            def step(m, c):
                to_group(m, later).wait_recv()
                relay(m, down, relay_send).start()
                relay(m, up, relay_two).start()

                @pl.when(y < ny - 1)
                def _():
                    h = m // half
                    r = lax.rem(m, half)
                    later[m] = times_map(earlier[m], h) + here[h * per_head + half + r]
                    to_group(m, later).start()

                return c

            lax.fori_loop(0, npe, step, 0)

    @pl.when(jnp.logical_and(jnp.logical_not(is_end), y > 0))
    def _():
        def step(m, c):
            relay(m, down, relay_send).wait_recv()

            @pl.when(z > mid)
            def _():
                relay(m, down, relay_send).start()

            @pl.when(z < mid - 1)
            def _():
                relay(m, up, relay_two).start()

            return c

        lax.fori_loop(0, npe, step, 0)

    @pl.when(z == 0)
    def _():
        for m in range(npe):
            entry_ref[m] = jnp.where(y > 0, earlier[m], 0.0)

    @pl.when(z > 0)
    def _():
        @pl.when(y == 0)
        def _():
            for m in range(npe):
                entry_ref[m] = before[(m // half) * per_head + half + m % half]

        @pl.when(y > 0)
        def _():
            split_maps(before)
            for m in range(npe):
                entry_ref[m] = (
                    times_map(earlier[m], m // half)
                    + before[(m // half) * per_head + half + m % half]
                )

    @pl.when(z < nz - 1)
    def _():
        def done(n, c):
            onward(n, own_ref).wait_send()
            return c

        lax.fori_loop(0, pieces, done, 0)

    @pl.when(jnp.logical_and(is_end, y < ny - 1))
    def _():
        def done(m, c):
            to_group(m, later).wait_send()
            return c

        lax.fori_loop(0, npe, done, 0)

    @pl.when(jnp.logical_and(y > 0, z > mid))
    def _():
        def done(m, c):
            relay(m, down, relay_send).wait_send()
            return c

        lax.fori_loop(0, npe, done, 0)

    @pl.when(jnp.logical_and(y > 0, jnp.logical_or(is_end, z < mid - 1)))
    def _():
        def done(m, c):
            relay(m, up, relay_two).wait_send()
            return c

        lax.fori_loop(0, npe, done, 0)


def state_chain(ns, nz, own):
    pieces = own.shape[0]
    nheads = pieces * ROWS // (2 * DK)
    npe = pieces // 2
    vm = pl.BlockSpec(memory_space=pltpu.VMEM)
    return pl.pallas_call(
        functools.partial(chain_kernel, ns, nz),
        name="state_chain",
        out_shape=jax.ShapeDtypeStruct((npe, ROWS, DK), F32),
        in_specs=[vm],
        out_specs=vm,
        scratch_shapes=[
            pltpu.VMEM((pieces, ROWS, DK), F32),
            pltpu.VMEM((pieces, ROWS, DK), F32),
            pltpu.VMEM((nheads, DK, DK), BF16),
            pltpu.VMEM((nheads, DK, DK), BF16),
            pltpu.VMEM((npe, ROWS, DK), F32),
            pltpu.VMEM((npe, ROWS, DK), F32),
            pltpu.SemaphoreType.DMA((pieces,)),
            pltpu.SemaphoreType.DMA((pieces,)),
            pltpu.SemaphoreType.DMA((npe,)),
            pltpu.SemaphoreType.DMA((npe,)),
            pltpu.SemaphoreType.DMA((npe,)),
            pltpu.SemaphoreType.DMA((npe,)),
        ],
        compiler_params=pltpu.CompilerParams(
            collective_id=1, has_side_effects=True, vmem_limit_bytes=VMEM_LIMIT
        ),
    )(own)


def output_kernel(qeff_ref, olocal_ref, entry_ref, gate_ref, gain_ref, weight_ref, part_ref, normed_s):
    nheads = qeff_ref.shape[1] // DK
    tokens = qeff_ref.shape[0]
    pieces = DV // ROWS
    step_rows = 128
    for h in range(nheads):
        entry = jnp.concatenate([entry_ref[h * pieces + r] for r in range(pieces)], axis=0)
        entry = halves(entry)
        lanes = slice(h * DV, (h + 1) * DV)

        def step(i, c):
            rows = pl.ds(pl.multiple_of(i * step_rows, step_rows), step_rows)
            core = olocal_ref[rows, lanes] + dot3(
                halves(qeff_ref[rows, lanes]), entry, ((1,), (1,))
            )
            scale = lax.rsqrt(jnp.mean(core * core, axis=1, keepdims=True) + norm_floor)
            gate = gate_ref[rows, lanes].astype(F32)
            gate = gate / (1.0 + jnp.exp(-gate))
            normed_s[rows, lanes] = (core * scale * gain_ref[...] * gate).astype(BF16)
            return c

        lax.fori_loop(0, tokens // step_rows, step, 0)

    wide = 256

    def project(i, c):
        rows = pl.ds(pl.multiple_of(i * wide, wide), wide)
        for j in range(weight_ref.shape[1] // wide):
            part_ref[rows, j * wide : (j + 1) * wide] = dot(
                normed_s[rows, :], weight_ref[:, j * wide : (j + 1) * wide]
            ).astype(BF16)
        return c

    lax.fori_loop(0, tokens // wide, project, 0)


def output_part(qeff, olocal, entry, gate, gain, weight):
    vm = pl.BlockSpec(memory_space=pltpu.VMEM)
    return pl.pallas_call(
        output_kernel,
        name="gated_projection",
        out_shape=jax.ShapeDtypeStruct((qeff.shape[0], weight.shape[1]), BF16),
        in_specs=[vm] * 6,
        out_specs=vm,
        scratch_shapes=[pltpu.VMEM((qeff.shape[0], weight.shape[0]), BF16)],
        compiler_params=pltpu.CompilerParams(vmem_limit_bytes=VMEM_LIMIT),
    )(qeff, olocal, entry, gate, gain, weight)


def sum_kernel(nh, part_ref, out_ref, twin, mine, landed, twin_send, twin_recv, send_sem, recv_sem):
    seq = lax.axis_index("seq")
    me = lax.axis_index("head")
    chips = nh // 2
    chip = me // 2
    core = lax.rem(me, 2)
    other = 1 - core
    rows = out_ref.shape[0]
    barrier = pltpu.get_barrier_semaphore()
    pl.semaphore_signal(barrier, inc=1, device_id=(seq, chip * 2 + other), device_id_type=MESH)
    for d in range(1, chips):
        pl.semaphore_signal(
            barrier, inc=1, device_id=(seq, lax.rem(chip + d, chips) * 2 + core), device_id_type=MESH
        )
    pl.semaphore_wait(barrier, chips)

    def block(d, side):
        start = (lax.rem(chip + d, chips) * 2 + side) * rows
        return pl.ds(pl.multiple_of(start, 64), rows)

    def to_twin(d):
        return pltpu.make_async_remote_copy(
            src_ref=part_ref.at[block(d, other), :],
            dst_ref=twin.at[d],
            send_sem=twin_send.at[d],
            recv_sem=twin_recv.at[d],
            device_id=(seq, chip * 2 + other),
            device_id_type=MESH,
        )

    def away(d):
        return pltpu.make_async_remote_copy(
            src_ref=mine.at[d],
            dst_ref=landed.at[d],
            send_sem=send_sem.at[d],
            recv_sem=recv_sem.at[d],
            device_id=(seq, lax.rem(chip + d, chips) * 2 + core),
            device_id_type=MESH,
        )

    order = [d for d in (2, 1, 3, 0) if d < chips]
    for d in order:
        to_twin(d).start()
    total = None
    for d in order:
        to_twin(d).wait_recv()
        both = part_ref[block(d, core), :].astype(F32) + twin[d].astype(F32)
        if d:
            mine[d] = both.astype(BF16)
            away(d).start()
        else:
            total = both
    for d in order:
        if d:
            away(d).wait_recv()
            total = total + landed[d].astype(F32)
    out_ref[...] = total.astype(BF16)
    for d in order:
        to_twin(d).wait_send()
        if d:
            away(d).wait_send()


def row_sums(nh, part):
    rows = part.shape[0] // nh
    width = part.shape[1]
    chips = nh // 2
    vm = pl.BlockSpec(memory_space=pltpu.VMEM)
    return pl.pallas_call(
        functools.partial(sum_kernel, nh),
        name="row_sums",
        out_shape=jax.ShapeDtypeStruct((rows, width), BF16),
        in_specs=[vm],
        out_specs=vm,
        scratch_shapes=[
            pltpu.VMEM((chips, rows, width), BF16),
            pltpu.VMEM((chips, rows, width), BF16),
            pltpu.VMEM((chips, rows, width), BF16),
            pltpu.SemaphoreType.DMA((chips,)),
            pltpu.SemaphoreType.DMA((chips,)),
            pltpu.SemaphoreType.DMA((chips,)),
            pltpu.SemaphoreType.DMA((chips,)),
        ],
        compiler_params=pltpu.CompilerParams(
            collective_id=2, has_side_effects=True, vmem_limit_bytes=VMEM_LIMIT
        ),
    )(part)


def on_device(
    ns, nh, query_input, key_input, value_input, gate_input, write_strength, log_decay,
    filter_query, filter_key, filter_value, norm_gain, out_weight,
):
    q, k, v, gate, ws, ld = exchange(
        ns, nh, (query_input, key_input, value_input, gate_input, write_strength, log_decay)
    )
    where = jnp.stack([lax.axis_index("seq"), lax.axis_index("head")]).astype(jnp.int32)
    own, qeff, olocal = local_terms(where, q, k, v, ws, ld, filter_query, filter_key, filter_value)
    entry = state_chain(ns, NZ, own)
    part = output_part(qeff, olocal, entry, gate, norm_gain.reshape(1, DV), out_weight)
    return row_sums(nh, part)


def solution(mesh):
    placed = (
        P(("seq", "head"), None),
        P(("seq", "head"), None),
        P(("seq", "head"), None),
        P(("seq", "head"), None),
        P(("seq", "head"), None),
        P(("seq", "head"), None),
        P(None, "head"),
        P(None, "head"),
        P(None, "head"),
        P(),
        P("head", None),
    )
    return jax.shard_map(
        functools.partial(on_device, mesh.shape["seq"], mesh.shape["head"]),
        mesh=mesh,
        in_specs=placed,
        out_specs=P(("seq", "head"), None),
        check_vma=False,
    )
```

time: 773 us -> 189 us (0.24)
  waiting for transfers between devices: 296 us -> 0 us
  other arithmetic: 190 us -> 0.55 us
  Pallas kernels: 0 us -> 184 us
  starting transfers between devices: 132 us -> 0 us
  matrix products: 92.2 us -> 0 us
  local copies, waits for them, and re-layouts: 40.2 us -> 4.44 us
  between operations: 13.8 us -> 0.03 us
    ppermute x32 -> x0, waiting for transfers between devices: 202 us -> none  [passed_along(): return lax.ppermute(value, axis, pairs)]
    pallas_call x0 -> x5, Pallas kernels: none -> 184 us  [the longest x1 67 us: local_terms(): pl.pallas_call(local_kernel, name='local_terms', out_shape=[jax.ShapeDtyp...]
    another operation x5 -> x1, other arithmetic: 161 us -> 0.55 us  [on_device(): jnp.stack([lax.axis_index('seq'), lax.axis_index('head')]).astype(jnp.int32)]
    ppermute x32 -> x0, starting transfers between devices: 103 us -> none  [passed_along(): return lax.ppermute(value, axis, pairs)]
    dot_general x70 -> x0, matrix products: 90.2 us -> none  [the longest x55 51.3 us: apply_maps(): return jnp.einsum('hde,hef->hdf', maps, states, precision=exact_mode)]
    reduce_scatter x1 -> x0, waiting for transfers between devices: 78.7 us -> none  [on_device(): lax.psum_scatter(jnp.dot(normed, out_weight, preferred_element_type=jnp.f...]
    all_to_all x6 -> x0, starting transfers between devices: 28.4 us -> none  [the longest x1 5 us: on_device(): lax.all_to_all(gate_input, 'head', split_axis=1, concat_axis=0, tiled=True)]
    while x86 -> x0, local copies, waits for them, and re-layouts: 17.3 us -> none
  transfers between devices with their start and end apart: 39 -> 0, of which waited for: 35 -> 0; matrix products, arithmetic and copies ran while one was open for 40% -> 0% of each run, Pallas kernels for 0% -> 0%
where the time goes in v1:
time: 189 us
  Pallas kernels  184 us (97%)
  local copies, waits for them, and re-layouts  4.44 us (2%)
    pallas_call x1, Pallas kernels, local_terms(): pl.pallas_call(local_kernel, name='local_terms', out_shape=[jax.ShapeDtyp...  67 us
    pallas_call x1, Pallas kernels, state_chain(): pl.pallas_call(functools.partial(chain_kernel, ns, nz), name='state_chain...  49.8 us
    pallas_call x1, Pallas kernels, row_sums(): pl.pallas_call(functools.partial(sum_kernel, nh), name='row_sums', out_sh...  29.9 us
    pallas_call x1, Pallas kernels, exchange(): pl.pallas_call(functools.partial(exchange_kernel, ns, nh), name='token_ex...  27.1 us
    pallas_call x1, Pallas kernels, output_part(): pl.pallas_call(output_kernel, name='gated_projection', out_shape=jax.Shap...  10.1 us
    unnamed x3, local copies, waits for them, and re-layouts  4.44 us

profile of v1, /device:TPU:121, one launch (start us, length us, event | category | flops | bytes accessed | tf_op | source)
XLA Modules:
  0.0 188.9 jit_solution(1920329392815769476)
XLA Ops:
  0.0 0.6 pad_add_fusion.where_ref
  0.6 1.4 copy.12.ws
  1.9 1.4 copy.13.ld
  3.3 27.1 %token_exchange.1 = (bf16[528,256]{1,0:T(8,128)(2,1)}, bf16[528,256]{1,0:T(8,128)(2,1)}, bf16[528,512]{1,0:T(8,128)(2,1)}, bf16[512,512]{1,0:T(8,128)(2,1)}, bf1...) custom-call(bf16[64,2048]{1,0:T(8,128)(2,1)} %q.1, bf16[64,2048]{1,0:T(8,128)(2,1)} %k.1, bf16[64,4096]{1,0:T(8,128)(2,1)} %v.1, ...), custom_call_target="tpu_custom_call" | custom-call | tf_op jit(solution)/shard_map/token_exchange/pallas_call | solution.py:143
  30.4 67.0 %local_terms.1 = (f32[16,64,128]{2,1,0:T(8,128)}, f32[512,512]{1,0:T(8,128)}, f32[512,512]{1,0:T(8,128)}) custom-call(s32[2]{0:T(128)} %pad_add_fusion.where_ref, bf16[528,256]{1,0:T(8,128)(2,1)} %get-tuple-element.14.q_ref, bf16[528,256]{1,0:T(8,128)(2,1)} %get-tuple-element.15.k_ref, bf16[528,512]{1,0:T(8,128)(2,1)} %get-tuple-element.16.v_ref, ...), custom_call_target="tpu_custom_call" | custom-call | tf_op jit(solution)/shard_map/local_terms/pallas_call | solution.py:319
  97.4 49.8 %state_chain.1.entry_ref = f32[8,64,128]{2,1,0:T(8,128)} custom-call(f32[16,64,128]{2,1,0:T(8,128)} %get-tuple-element.21.own_ref), custom_call_target="tpu_custom_call" | custom-call | tf_op jit(solution)/shard_map/state_chain/pallas_call | solution.py:559
  147.2 10.1 %gated_projection.1.part_ref = bf16[512,2048]{1,0:T(8,128)(2,1)} custom-call(f32[512,512]{1,0:T(8,128)} %get-tuple-element.19.qeff_ref, f32[512,512]{1,0:T(8,128)} %get-tuple-element.20.olocal_ref, f32[8,64,128]{2,1,0:T(8,128)} %state_chain.1.entry_ref, bf16[512,512]{1,0:T(8,128)(2,1)} %get-tuple-element.22.gate_ref, f32[1,128]{1,0:T(1,128)} %bitcast.3, ...), custom_call_target="tpu_custom_call" | custom-call | tf_op jit(solution)/shard_map/gated_projection/pallas_call | solution.py:623
  157.3 29.9 %row_sums.1 = bf16[64,2048]{1,0:T(8,128)(2,1)} custom-call(bf16[512,2048]{1,0:T(8,128)(2,1)} %gated_projection.1.part_ref), custom_call_target="tpu_custom_call" | custom-call | tf_op jit(solution)/shard_map/row_sums/pallas_call | solution.py:702
  187.3 1.7 copy.15

commit v2 on v1

v2 whole, which is shorter than its diff:
```python
import functools

import jax
import jax.numpy as jnp
from jax import lax
from jax.experimental import pallas as pl
from jax.experimental.pallas import tpu as pltpu
from jax.sharding import PartitionSpec as P

HK = 16
HV = 32
DK = 128
DV = 128
CH = 64
PAD = 16
NZ = 8
ROWS = 64
norm_floor = 1e-06
F32 = jnp.float32
BF16 = jnp.bfloat16
MESH = pl.DeviceIdType.MESH
VMEM_LIMIT = 60 * 1024 * 1024


def halves(x):
    high = x.astype(BF16)
    low = (x - high.astype(F32)).astype(BF16)
    return high, low


def dot(a, b, dims=((1,), (0,))):
    return lax.dot_general(a, b, (dims, ((), ())), preferred_element_type=F32)


def dot3(a, b, dims=((1,), (0,))):
    ah, al = a
    bh, bl = b
    return dot(ah, bh, dims) + (dot(ah, bl, dims) + dot(al, bh, dims))


def exchange_kernel(
    ns, nh, via, q, k, v, wl, qo, ko, vo, wlo, rq, rk, rv,
    send_sem, recv_sem, hop_send, hop_recv, pass_send, pass_recv, halo_send, halo_recv, own_sem,
):
    seq = lax.axis_index("seq")
    me = lax.axis_index("head")
    rows = q.shape[0]
    chips = nh // 2
    chip = me // 2
    odd = lax.rem(me, 2) == 1
    ins = (q, k, v, wl)
    outs = (qo, ko, vo, wlo)
    pads = (PAD, PAD, PAD, 0)
    hops = (rq, rk, rv)
    nbr = lax.rem(chip + via, chips) * 2 + 1
    far = lax.rem(chip + 2, chips)
    next_far = lax.rem(chip + via, chips)
    origin = lax.rem(chip + chips - via, chips) * 2 + 1
    last = jnp.logical_and(me == nh - 1, seq < ns - 1)
    barrier = pltpu.get_barrier_semaphore()
    for d in range(1, nh):
        pl.semaphore_signal(
            barrier, inc=1, device_id=(seq, lax.rem(me + d, nh)), device_id_type=MESH
        )

    @pl.when(seq > 0)
    def _():
        pl.semaphore_signal(barrier, inc=1, device_id=(seq - 1, nh - 1), device_id_type=MESH)

    @pl.when(last)
    def _():
        for d in range(nh):
            pl.semaphore_signal(barrier, inc=1, device_id=(seq + 1, d), device_id_type=MESH)

    def piece(a, who):
        if a == 3:
            return ins[a]
        width = outs[a].shape[1]
        return ins[a].at[:, pl.ds(pl.multiple_of(who * width, width), width)]

    def place(a, who):
        return outs[a].at[pl.ds(pl.multiple_of(pads[a] + who * rows, 16), rows), :]

    def own(a):
        return pltpu.make_async_copy(piece(a, me), place(a, me), own_sem.at[a])

    for a in range(4):
        own(a).start()
    pl.semaphore_wait(barrier, nh - 1 + jnp.where(seq > 0, 1, 0) + jnp.where(last, nh, 0))

    def across(d, a, to, source):
        return pltpu.make_async_remote_copy(
            src_ref=piece(a, to),
            dst_ref=place(a, source),
            send_sem=send_sem.at[d - 1, a],
            recv_sem=recv_sem.at[d - 1, a],
            device_id=(seq, to),
            device_id_type=MESH,
        )

    def halo(d, a):
        width = outs[a].shape[1]
        return pltpu.make_async_remote_copy(
            src_ref=ins[a].at[pl.ds(rows - PAD, PAD), pl.ds(d * width, width)],
            dst_ref=outs[a].at[pl.ds(0, PAD), :],
            send_sem=halo_send.at[d, a],
            recv_sem=halo_recv.at[a],
            device_id=(seq + 1, d),
            device_id_type=MESH,
        )

    def hop(side, a):
        return pltpu.make_async_remote_copy(
            src_ref=piece(a, far * 2 + side),
            dst_ref=hops[a].at[side],
            send_sem=hop_send.at[side, a],
            recv_sem=hop_recv.at[side, a],
            device_id=(seq, nbr),
            device_id_type=MESH,
        )

    def passed(side, a):
        return pltpu.make_async_remote_copy(
            src_ref=hops[a].at[side],
            dst_ref=place(a, origin),
            send_sem=pass_send.at[side, a],
            recv_sem=pass_recv.at[a],
            device_id=(seq, next_far * 2 + side),
            device_id_type=MESH,
        )

    @pl.when(last)
    def _():
        for d in range(nh):
            for a in range(3):
                halo(d, a).start()

    def target(d):
        return lax.rem(me + d, nh)

    def source(d):
        return lax.rem(me + nh - d, nh)

    @pl.when(odd)
    def _():
        for a in range(3):
            for side in range(2):
                hop(side, a).start()
        for d in (3, 4):
            across(d, 3, target(d), me).start()
        for a in (3, 0, 1, 2):
            for d in (2, 6, 5, 1, 7):
                across(d, a, target(d), me).start()

    @pl.when(jnp.logical_not(odd))
    def _():
        for a in (3, 0, 1, 2):
            for d in (4, 5, 2, 6, 3, 1, 7):
                across(d, a, target(d), me).start()

    @pl.when(odd)
    def _():
        for a in range(3):
            for side in range(2):
                hop(side, a).wait_recv()
                passed(side, a).start()

    for a in range(3):
        passed(0, a).wait_recv()

    @pl.when(odd)
    def _():
        for d in range(1, nh):
            for a in range(4):
                if d == 4 and a < 3:
                    continue
                across(d, a, target(d), source(d)).wait_recv()
        for d in range(1, nh):
            for a in range(4):
                if d in (3, 4) and a < 3:
                    continue
                across(d, a, target(d), source(d)).wait_send()
        for a in range(3):
            for side in range(2):
                hop(side, a).wait_send()
                passed(side, a).wait_send()

    @pl.when(jnp.logical_not(odd))
    def _():
        for d in range(1, nh):
            for a in range(4):
                if not (d == 3 and a < 3):
                    across(d, a, target(d), source(d)).wait_recv()
                across(d, a, target(d), source(d)).wait_send()

    @pl.when(seq > 0)
    def _():
        for a in range(3):
            halo(0, a).wait_recv()

    @pl.when(last)
    def _():
        for d in range(nh):
            for a in range(3):
                halo(d, a).wait_send()

    for a in range(4):
        own(a).wait()


VIA = 3


def exchange(ns, nh, arrays):
    rows = arrays[0].shape[0]
    total = rows * nh
    shapes = []
    for i, x in enumerate(arrays):
        width = x.shape[1] // nh if i < 3 else x.shape[1]
        shapes.append(jax.ShapeDtypeStruct((total + (PAD if i < 3 else 0), width), x.dtype))
    return pl.pallas_call(
        functools.partial(exchange_kernel, ns, nh, VIA),
        name="token_exchange",
        out_shape=shapes,
        in_specs=[pl.BlockSpec(memory_space=pl.ANY)] * 4,
        out_specs=[pl.BlockSpec(memory_space=pltpu.VMEM)] * 4,
        scratch_shapes=[pltpu.VMEM((2, rows, s.shape[1]), BF16) for s in shapes[:3]]
        + [
            pltpu.SemaphoreType.DMA((nh - 1, 4)),
            pltpu.SemaphoreType.DMA((nh - 1, 4)),
            pltpu.SemaphoreType.DMA((2, 3)),
            pltpu.SemaphoreType.DMA((2, 3)),
            pltpu.SemaphoreType.DMA((2, 3)),
            pltpu.SemaphoreType.DMA((3,)),
            pltpu.SemaphoreType.DMA((nh, 3)),
            pltpu.SemaphoreType.DMA((3,)),
            pltpu.SemaphoreType.DMA((4,)),
        ],
        compiler_params=pltpu.CompilerParams(
            collective_id=0, has_side_effects=True, vmem_limit_bytes=VMEM_LIMIT
        ),
    )(*arrays)


def local_kernel(
    q_ref, k_ref, v_ref, wl_ref, fq_ref, fk_ref, fv_ref,
    chain_ref, qeff_ref, olocal_ref,
    key_s, query_s, w_s, e_s, mix_s, low_s, flip_s, sol_s, inv_s, value_s,
    grow_s, tail_s, gamma_s, right_s, turned_s, state_s,
):
    seq = lax.axis_index("seq")
    head = lax.axis_index("head")
    tokens = wl_ref.shape[0]
    blocks = tokens // CH
    nheads = v_ref.shape[1] // DV
    nkeys = k_ref.shape[1] // DK
    share = nheads // nkeys
    sets = blocks * nkeys
    both = share * CH
    row = lax.broadcasted_iota(jnp.int32, (CH, both), 0)
    lane = lax.broadcasted_iota(jnp.int32, (CH, both), 1)
    col = lax.rem(lane, CH)
    second_head = lane >= CH
    incl = col <= row
    strict = col < row
    lower_ones = (
        lax.broadcasted_iota(jnp.int32, (CH, CH), 1) <= lax.broadcasted_iota(jnp.int32, (CH, CH), 0)
    ).astype(F32).astype(BF16)
    upper_ones = (row <= col).astype(F32).astype(BF16)
    copies = (row == col).astype(F32).astype(BF16)
    allh = wl_ref.shape[1] // 2
    pick = (
        lax.broadcasted_iota(jnp.int32, (allh, 128), 0)
        == head * nheads + lax.broadcasted_iota(jnp.int32, (allh, 128), 1)
    )
    pick = jnp.logical_and(pick, lax.broadcasted_iota(jnp.int32, (allh, 128), 1) < nheads)
    pick = pick.astype(F32).astype(BF16)
    pick_t = (
        lax.broadcasted_iota(jnp.int32, (8, allh), 1)
        == head * nheads + lax.broadcasted_iota(jnp.int32, (8, allh), 0)
    )
    pick_t = jnp.logical_and(pick_t, lax.broadcasted_iota(jnp.int32, (8, allh), 0) < nheads)
    pick_t = pick_t.astype(F32).astype(BF16)

    def filtered(ref, taps, start, lo, width):
        x = ref[pl.ds(start, CH + PAD), lo : lo + width].astype(F32)
        edge = lax.broadcasted_iota(jnp.int32, (CH + PAD, width), 0) < PAD
        x = jnp.where(jnp.logical_and(edge, jnp.logical_and(seq == 0, start == 0)), 0.0, x)
        total = None
        for j in range(4):
            term = taps[j : j + 1, lo : lo + width].astype(F32) * x[PAD - 3 + j : PAD - 3 + j + CH]
            total = term if total is None else total + term
        return total / (1.0 + jnp.exp(-total))

    def gather_terms(c, carry):
        start = pl.multiple_of(c * CH, CH)
        rows = pl.ds(start, CH)
        wsc = wl_ref[rows, :allh]
        ldc = wl_ref[rows, allh:]
        beta_c = dot(wsc, pick)
        dec_c = dot(ldc, pick)
        beta_r = dot(dot(pick_t, wsc, ((1,), (1,))).astype(BF16), copies)
        dec_r = dot(pick_t, ldc, ((1,), (1,)))
        cum_c = dot(lower_ones, dec_c.astype(BF16))
        cum_r = dot(dec_r.astype(BF16), upper_ones)
        grow_c = jnp.exp(cum_c)
        gamma = grow_c[CH - 1 : CH, :]
        gamma_s[pl.ds(pl.multiple_of(c * 8, 8), 8), :] = jnp.broadcast_to(gamma, (8, 128))
        grow_s[rows, :] = grow_c
        tail_s[pl.ds(pl.multiple_of(c * 8, 8), 8), :] = jnp.exp(cum_r[:, CH - 1 : CH] - cum_r)
        for p in range(nkeys):
            lanes = slice(p * DK, (p + 1) * DK)
            key = filtered(k_ref, fk_ref, start, p * DK, DK)
            key = key * lax.rsqrt(jnp.sum(key * key, axis=1, keepdims=True) + norm_floor)
            query = filtered(q_ref, fq_ref, start, p * DK, DK)
            query = query * (
                lax.rsqrt(jnp.sum(query * query, axis=1, keepdims=True) + norm_floor) * DK ** (-0.5)
            )
            key_s[rows, lanes] = key
            query_s[rows, lanes] = query
            kh, kl = halves(key)
            twice = tuple(jnp.concatenate([t] * share, axis=0) for t in (kh, kl))
            kk = dot3((kh, kl), twice, ((1,), (1,)))
            qk = dot3(halves(query), twice, ((1,), (1,)))
            h = p * share

            at = pl.ds(pl.multiple_of((c * nkeys + p) * CH, CH), CH)
            lowers = []
            for s in range(share):
                spread = cum_c[:, h + s : h + s + 1] - cum_r[h + s : h + s + 1, :]
                ratios = jnp.where(incl, jnp.exp(jnp.where(incl, spread, 0.0)), 0.0)
                mix_s[h + s, rows, :] = qk * ratios
                lowers.append(beta_c[:, h + s : h + s + 1] * kk * ratios)
            low_s[at, :] = jnp.where(strict, jnp.where(second_head, lowers[1], lowers[0]), 0.0)
            turned_s[pl.ds(pl.multiple_of((c * nkeys + p) * DK, DK), DK), :] = jnp.concatenate(
                [key] * share, axis=0
            ).T
            right = jnp.where(second_head[:1], beta_r[h + 1 : h + 2, :], beta_r[h : h + 1, :])
            grown = right * jnp.exp(
                jnp.where(second_head[:1], cum_r[h + 1 : h + 2, :], cum_r[h : h + 1, :])
            )
            right_s[pl.ds(pl.multiple_of((c * nkeys + p) * 8, 8), 8), :] = jnp.concatenate(
                [jnp.broadcast_to(right, (4, both)), jnp.broadcast_to(grown, (4, both))], axis=0
            )
            for s in range(share):
                hv = slice((h + s) * DV, (h + s + 1) * DV)
                value_s[rows, hv] = filtered(v_ref, fv_ref, start, (h + s) * DV, DV)
        return carry

    lax.fori_loop(0, blocks, gather_terms, 0, unroll=2)

    copies_n = 128 // sets
    groups = copies_n // share
    width = CH // groups
    lane_h = lax.rem(lax.broadcasted_iota(jnp.int32, (CH, 128), 1) // sets, share) == 1

    def turn(i, carry):
        x = low_s[pl.ds(i, sets, stride=CH), :]
        t = jnp.concatenate([x] * copies_n, axis=0).T
        flip_s[i] = jnp.where(lane_h, t[CH:], t[:CH])
        return carry

    lax.fori_loop(0, CH, turn, 0, unroll=8)
    place = lax.broadcasted_iota(jnp.int32, (width, 128), 0) + width * (
        lax.broadcasted_iota(jnp.int32, (width, 128), 1) // (sets * share)
    )

    def solve(b, carry):
        base = b * 8
        accs = tuple(jnp.where(place == base + r, 1.0, 0.0) for r in range(8))

        def inner(jb, accs):
            accs = list(accs)
            start = pl.multiple_of(jb * 8, 8)
            tiles = [flip_s[base + r, pl.ds(start, 8), :] for r in range(8)]
            for jj in range(8):
                t = sol_s[start + jj]
                for r in range(8):
                    accs[r] = accs[r] - tiles[r][jj : jj + 1] * t
            return tuple(accs)

        accs = list(lax.fori_loop(0, b, inner, accs))
        tiles = [flip_s[base + r, pl.ds(pl.multiple_of(base, 8), 8), :] for r in range(8)]
        for r in range(8):
            sol_s[base + r] = accs[r]
            for later in range(r + 1, 8):
                accs[later] = accs[later] - tiles[later][r : r + 1] * accs[r]
        return carry

    lax.fori_loop(0, CH // 8, solve, 0)
    from_row = lax.broadcasted_iota(jnp.int32, (128, 128), 0)
    from_lane = lax.broadcasted_iota(jnp.int32, (128, 128), 1)
    matching = jnp.logical_and(
        from_row // CH == lax.rem(from_lane // sets, share),
        lax.rem(from_row, CH) // width == from_lane // (sets * share),
    )

    def turn_back(i, carry):
        x = jnp.where(matching, jnp.concatenate([sol_s[i]] * copies_n, axis=0), 0.0).T
        total = x[:sets]
        for r in range(1, copies_n):
            total = total + x[r * sets : (r + 1) * sets]
        inv_s[pl.ds(i, sets, stride=CH), :] = total
        return carry

    lax.fori_loop(0, CH, turn_back, 0, unroll=8)

    def applied(c, carry):
        rows = pl.ds(pl.multiple_of(c * CH, CH), CH)
        for p in range(nkeys):
            at = pl.ds(pl.multiple_of((c * nkeys + p) * CH, CH), CH)
            inv = inv_s[at, :]
            right = right_s[pl.ds(pl.multiple_of((c * nkeys + p) * 8, 8), 8), :]
            h = p * share
            for source, out, r in ((value_s, w_s, 0), (key_s, e_s, 4)):
                left = halves(inv * right[r : r + 1, :])
                if r == 0:
                    parts = [halves(source[rows, (h + s) * DV : (h + s + 1) * DV]) for s in range(share)]
                else:
                    parts = [halves(source[rows, p * DK : (p + 1) * DK])] * share
                zero = jnp.zeros((CH, DV), BF16)
                wide = tuple(
                    jnp.concatenate(
                        [
                            jnp.concatenate([parts[0][i], zero], axis=1),
                            jnp.concatenate([zero, parts[1][i]], axis=1),
                        ],
                        axis=0,
                    )
                    for i in range(2)
                )
                out[rows, h * DV : (h + share) * DV] = dot3(left, wide)
        return carry

    lax.fori_loop(0, blocks, applied, 0, unroll=4)

    eye_k = (
        lax.broadcasted_iota(jnp.int32, (DK, DK + DV), 0)
        == lax.broadcasted_iota(jnp.int32, (DK, DK + DV), 1)
    ).astype(F32)
    for h in range(nheads):
        state_s[h] = eye_k

    def second(c, carry):
        start = pl.multiple_of(c * CH, CH)
        rows = pl.ds(start, CH)
        grow_c = grow_s[rows, :]
        tail_r = tail_s[pl.ds(pl.multiple_of(c * 8, 8), 8), :]
        gamma = gamma_s[pl.ds(pl.multiple_of(c * 8, 8), 8), :]
        for h in range(nheads):
            p = h // share
            query = query_s[rows, p * DK : (p + 1) * DK]
            state = state_s[h]
            sh, sl = halves(state)
            e = e_s[rows, h * DK : (h + 1) * DK]
            w = w_s[rows, h * DV : (h + 1) * DV]
            lh, ll = halves(jnp.concatenate([e, query * grow_c[:, h : h + 1]], axis=0))
            x = dot(
                jnp.concatenate([lh, ll], axis=1), jnp.concatenate([sh, sh], axis=0)
            ) + dot(lh, sl)
            fresh = jnp.concatenate([-x[:CH, :DK], w - x[:CH, DK:]], axis=1)
            fr = halves(fresh)
            turned = turned_s[pl.ds(pl.multiple_of((c * nkeys + p) * DK, DK), DK), :]
            left = jnp.concatenate([mix_s[h, rows, :], turned * tail_r[h : h + 1, :]], axis=0)
            y = dot(jnp.concatenate(halves(left), axis=1), jnp.concatenate(fr + fr, axis=0))
            state_s[h] = gamma[0:1, h : h + 1] * state + y[CH:]
            y = x[CH:] + y[:CH]
            qeff_ref[rows, h * DK : (h + 1) * DK] = y[:, :DK]
            olocal_ref[rows, h * DV : (h + 1) * DV] = y[:, DK:]
        return carry

    lax.fori_loop(0, blocks, second, 0, unroll=4)
    for h in range(nheads):
        for part in range(2):
            t = state_s[h, :, part * DK : (part + 1) * DK].T
            for r in range(DK // ROWS):
                chain_ref[h * 2 * (DK // ROWS) + part * (DK // ROWS) + r] = t[
                    r * ROWS : (r + 1) * ROWS
                ]


def local_terms(q, k, v, wl, fq, fk, fv):
    tokens = wl.shape[0]
    nheads = v.shape[1] // DV
    nkeys = k.shape[1] // DK
    vm = pl.BlockSpec(memory_space=pltpu.VMEM)
    return pl.pallas_call(
        local_kernel,
        name="local_terms",
        out_shape=[
            jax.ShapeDtypeStruct((nheads * 2 * DK // ROWS, ROWS, DK), F32),
            jax.ShapeDtypeStruct((tokens, nheads * DK), F32),
            jax.ShapeDtypeStruct((tokens, nheads * DV), F32),
        ],
        in_specs=[vm] * 7,
        out_specs=[vm] * 3,
        scratch_shapes=[
            pltpu.VMEM((tokens, nkeys * DK), F32),
            pltpu.VMEM((tokens, nkeys * DK), F32),
            pltpu.VMEM((tokens, nheads * DV), F32),
            pltpu.VMEM((tokens, nheads * DK), F32),
            pltpu.VMEM((nheads, tokens, 2 * CH), F32),
            pltpu.VMEM((tokens * nkeys, 2 * CH), F32),
            pltpu.VMEM((CH, CH, 128), F32),
            pltpu.VMEM((CH, 16, 128), F32),
            pltpu.VMEM((tokens * nkeys, 2 * CH), F32),
            pltpu.VMEM((tokens, nheads * DV), F32),
            pltpu.VMEM((tokens, 128), F32),
            pltpu.VMEM((tokens // CH * 8, 128), F32),
            pltpu.VMEM((tokens // CH * 8, 128), F32),
            pltpu.VMEM((tokens // CH * nkeys * 8, 2 * CH), F32),
            pltpu.VMEM((tokens // CH * nkeys * DK, 2 * CH), F32),
            pltpu.VMEM((nheads, DK, DK + DV), F32),
        ],
        compiler_params=pltpu.CompilerParams(vmem_limit_bytes=VMEM_LIMIT),
    )(q, k, v, wl, fq, fk, fv)


def chain_kernel(
    ns, nh, nz, own_ref, gate_in, entry_ref, gate_ref,
    before, here, map_h, map_l, pre_h, pre_l, tot_h, tot_l, earlier, later,
    pre_send, pre_recv, far_send, far_recv, relay_send, relay_two, gate_send, gate_recv, gate_own,
):
    seq = lax.axis_index("seq")
    head = lax.axis_index("head")
    ny = ns // nz
    z = lax.rem(seq, nz)
    y = seq // nz
    pieces = own_ref.shape[0]
    per_head = 2 * DK // ROWS
    half = per_head // 2
    nheads = pieces // per_head
    npe = nheads * half
    base = y * nz
    up = base + lax.rem(z + 1, nz)
    down = base + lax.rem(z + nz - 1, nz)
    mid = nz // 2
    is_end = z == nz - 1
    rows = gate_in.shape[0]
    width = gate_ref.shape[1]

    barrier = pltpu.get_barrier_semaphore()
    for other in (up, down):
        pl.semaphore_signal(barrier, inc=1, device_id=(other, head), device_id_type=MESH)
    for d in range(1, nh):
        pl.semaphore_signal(
            barrier, inc=1, device_id=(seq, lax.rem(head + d, nh)), device_id_type=MESH
        )

    @pl.when(jnp.logical_and(is_end, y > 0))
    def _():
        pl.semaphore_signal(barrier, inc=1, device_id=(seq - nz, head), device_id_type=MESH)

    @pl.when(jnp.logical_and(is_end, y < ny - 1))
    def _():
        pl.semaphore_signal(barrier, inc=1, device_id=(seq + nz, head), device_id_type=MESH)

    def gate_piece(who):
        return gate_in.at[:, pl.ds(pl.multiple_of(who * width, width), width)]

    def gate_place(who):
        return gate_ref.at[pl.ds(pl.multiple_of(who * rows, 16), rows), :]

    def gate_across(d, to, source):
        return pltpu.make_async_remote_copy(
            src_ref=gate_piece(to),
            dst_ref=gate_place(source),
            send_sem=gate_send.at[d - 1],
            recv_sem=gate_recv.at[d - 1],
            device_id=(seq, to),
            device_id_type=MESH,
        )

    gate_mine = pltpu.make_async_copy(gate_piece(head), gate_place(head), gate_own)
    gate_mine.start()
    for h in range(nheads):
        for r in range(half):
            hi, lo = halves(own_ref[h * per_head + r])
            map_h[h, r * ROWS : (r + 1) * ROWS, :] = hi
            map_l[h, r * ROWS : (r + 1) * ROWS, :] = lo
    pl.semaphore_wait(
        barrier,
        1
        + nh
        + jnp.where(jnp.logical_and(is_end, y > 0), 1, 0)
        + jnp.where(jnp.logical_and(is_end, y < ny - 1), 1, 0),
    )

    def onward(n, source):
        return pltpu.make_async_remote_copy(
            src_ref=source.at[n],
            dst_ref=before.at[n],
            send_sem=pre_send.at[n],
            recv_sem=pre_recv.at[n],
            device_id=(up, head),
            device_id_type=MESH,
        )

    def to_group(m, source):
        return pltpu.make_async_remote_copy(
            src_ref=source.at[m],
            dst_ref=earlier.at[m],
            send_sem=far_send.at[m],
            recv_sem=far_recv.at[m],
            device_id=(seq + nz, head),
            device_id_type=MESH,
        )

    def relay(m, to, sem):
        return pltpu.make_async_remote_copy(
            src_ref=earlier.at[m],
            dst_ref=earlier.at[m],
            send_sem=sem.at[m],
            recv_sem=far_recv.at[m],
            device_id=(to, head),
            device_id_type=MESH,
        )

    @pl.when(z == 0)
    def _():
        def send(n, c):
            onward(n, own_ref).start()
            return c

        lax.fori_loop(0, pieces, send, 0)

    for d in range(1, nh):
        gate_across(d, lax.rem(head + d, nh), head).start()

    def prefix(h, part):
        n = h * per_head + part
        onward(n, here).wait_recv()
        xh, xl = halves(before[n])
        if part < half:
            pre_h[h, part * ROWS : (part + 1) * ROWS, :] = xh
            pre_l[h, part * ROWS : (part + 1) * ROWS, :] = xl
        r = dot3((xh, xl), (map_h[h], map_l[h]))
        if part >= half:
            r = r + own_ref[n]
        here[n] = r

    def corrected(m, h, r):
        entry_ref[m] = (
            dot3(halves(earlier[m]), (pre_h[h], pre_l[h])) + before[h * per_head + half + r]
        )

    @pl.when(jnp.logical_and(z > 0, z < nz - 1))
    def _():
        def step(h, c):
            for part in range(per_head):
                prefix(h, part)
                onward(h * per_head + part, here).start()
            return c

        lax.fori_loop(0, nheads, step, 0)

    @pl.when(is_end)
    def _():
        def step(h, c):
            for part in range(per_head):
                prefix(h, part)

            @pl.when(y == 0)
            def _():
                for r in range(half):
                    m = h * half + r
                    later[m] = here[h * per_head + half + r]
                    to_group(m, later).start()

            @pl.when(y > 0)
            def _():
                for r in range(half):
                    hi, lo = halves(here[h * per_head + r])
                    tot_h[h, r * ROWS : (r + 1) * ROWS, :] = hi
                    tot_l[h, r * ROWS : (r + 1) * ROWS, :] = lo
                for r in range(half):
                    m = h * half + r
                    to_group(m, later).wait_recv()
                    relay(m, down, relay_send).start()
                    relay(m, up, relay_two).start()

                    @pl.when(y < ny - 1)
                    def _():
                        later[m] = (
                            dot3(halves(earlier[m]), (tot_h[h], tot_l[h]))
                            + here[h * per_head + half + r]
                        )
                        to_group(m, later).start()

                for r in range(half):
                    corrected(h * half + r, h, r)

            return c

        lax.fori_loop(0, nheads, step, 0)

    @pl.when(jnp.logical_and(jnp.logical_not(is_end), y > 0))
    def _():
        def step(h, c):
            for r in range(half):
                m = h * half + r
                relay(m, down, relay_send).wait_recv()

                @pl.when(z > mid)
                def _():
                    relay(m, down, relay_send).start()

                @pl.when(z < mid - 1)
                def _():
                    relay(m, up, relay_two).start()

                @pl.when(z == 0)
                def _():
                    entry_ref[m] = earlier[m]

                @pl.when(z > 0)
                def _():
                    corrected(m, h, r)

            return c

        lax.fori_loop(0, nheads, step, 0)

    @pl.when(y == 0)
    def _():
        @pl.when(z == 0)
        def _():
            entry_ref[...] = jnp.zeros_like(entry_ref)

        @pl.when(z > 0)
        def _():
            for m in range(npe):
                entry_ref[m] = before[(m // half) * per_head + half + m % half]

    @pl.when(z < nz - 1)
    def _():
        def done(n, c):
            onward(n, own_ref).wait_send()
            return c

        lax.fori_loop(0, pieces, done, 0)

    @pl.when(jnp.logical_and(is_end, y < ny - 1))
    def _():
        def done(m, c):
            to_group(m, later).wait_send()
            return c

        lax.fori_loop(0, npe, done, 0)

    @pl.when(jnp.logical_and(y > 0, z > mid))
    def _():
        def done(m, c):
            relay(m, down, relay_send).wait_send()
            return c

        lax.fori_loop(0, npe, done, 0)

    @pl.when(jnp.logical_and(y > 0, jnp.logical_or(is_end, z < mid - 1)))
    def _():
        def done(m, c):
            relay(m, up, relay_two).wait_send()
            return c

        lax.fori_loop(0, npe, done, 0)

    gate_mine.wait()
    for d in range(1, nh):
        gate_across(d, lax.rem(head + d, nh), lax.rem(head + nh - d, nh)).wait()


def state_chain(ns, nh, nz, own, gate):
    pieces = own.shape[0]
    nheads = pieces * ROWS // (2 * DK)
    npe = pieces // 2
    vm = pl.BlockSpec(memory_space=pltpu.VMEM)
    return pl.pallas_call(
        functools.partial(chain_kernel, ns, nh, nz),
        name="state_chain",
        out_shape=[
            jax.ShapeDtypeStruct((npe, ROWS, DK), F32),
            jax.ShapeDtypeStruct((gate.shape[0] * nh, gate.shape[1] // nh), gate.dtype),
        ],
        in_specs=[vm, pl.BlockSpec(memory_space=pl.ANY)],
        out_specs=[vm, vm],
        scratch_shapes=[pltpu.VMEM((pieces, ROWS, DK), F32)] * 2
        + [pltpu.VMEM((nheads, DK, DK), BF16)] * 6
        + [pltpu.VMEM((npe, ROWS, DK), F32)] * 2
        + [pltpu.SemaphoreType.DMA((pieces,))] * 2
        + [pltpu.SemaphoreType.DMA((npe,))] * 4
        + [pltpu.SemaphoreType.DMA((nh - 1,))] * 2
        + [pltpu.SemaphoreType.DMA],
        compiler_params=pltpu.CompilerParams(
            collective_id=1, has_side_effects=True, vmem_limit_bytes=VMEM_LIMIT
        ),
    )(own, gate)


def output_kernel(
    nh, qeff_ref, olocal_ref, entry_ref, gate_ref, gain_ref, weight_ref, out_ref,
    normed_s, own_s, twin_out, twin_in, gone, landed, twin_send, twin_recv, send_sem, recv_sem,
):
    seq = lax.axis_index("seq")
    me = lax.axis_index("head")
    nheads = qeff_ref.shape[1] // DK
    chips = nh // 2
    chip = me // 2
    core = lax.rem(me, 2)
    other = 1 - core
    rows = out_ref.shape[0]
    ahead = lax.rem(chip + 1 + 2 * core, chips)
    behind = lax.rem(chip + 3 + 2 * core, chips)
    fwd = 1 + 2 * core
    bwd = 3 - 2 * core
    barrier = pltpu.get_barrier_semaphore()
    pl.semaphore_signal(barrier, inc=1, device_id=(seq, chip * 2 + other), device_id_type=MESH)
    for to in (ahead, behind):
        pl.semaphore_signal(barrier, inc=1, device_id=(seq, to * 2 + core), device_id_type=MESH)

    pieces = DV // ROWS
    entries = []
    for h in range(nheads):
        entry = jnp.concatenate([entry_ref[h * pieces + r] for r in range(pieces)], axis=0)
        entries.append(halves(entry))

    def normalized(d):
        start = pl.multiple_of(lax.rem(chip + d, chips) * (2 * rows), 2 * rows)
        at = pl.ds(start, 2 * rows)
        for h in range(nheads):
            lanes = slice(h * DV, (h + 1) * DV)
            core_out = olocal_ref[at, lanes] + dot3(
                halves(qeff_ref[at, lanes]), entries[h], ((1,), (1,))
            )
            scale = lax.rsqrt(jnp.mean(core_out * core_out, axis=1, keepdims=True) + norm_floor)
            gate = gate_ref[at, lanes].astype(F32)
            gate = gate / (1.0 + jnp.exp(-gate))
            normed_s[:, lanes] = (core_out * scale * gain_ref[...] * gate).astype(BF16)

    def to_twin(d):
        return pltpu.make_async_remote_copy(
            src_ref=twin_out.at[d],
            dst_ref=twin_in.at[d],
            send_sem=twin_send.at[d],
            recv_sem=twin_recv.at[d],
            device_id=(seq, chip * 2 + other),
            device_id_type=MESH,
        )

    def away(i, to):
        return pltpu.make_async_remote_copy(
            src_ref=gone.at[i],
            dst_ref=landed.at[i],
            send_sem=send_sem.at[i],
            recv_sem=recv_sem.at[i],
            device_id=(seq, to * 2 + core),
            device_id_type=MESH,
        )

    wide = 512
    nwide = weight_ref.shape[1] // wide
    mine_at = pl.ds(pl.multiple_of(core * rows, rows), rows)
    other_at = pl.ds(pl.multiple_of(other * rows, rows), rows)

    def project(d):
        normalized(d)
        for j in range(nwide):
            lanes = slice(j * wide, (j + 1) * wide)
            twin_out[d, :, lanes] = dot(normed_s[other_at, :], weight_ref[:, lanes]).astype(BF16)
            own_s[d, :, lanes] = dot(normed_s[mine_at, :], weight_ref[:, lanes])

    def pair_sum(d):
        return own_s[d] + twin_in[d].astype(F32)

    order = (2, 1, 3, 0)
    for i, d in enumerate(order):
        project(d)
        if i == 0:
            pl.semaphore_wait(barrier, 3)
        to_twin(d).start()
        if d == 1:
            to_twin(2).wait_recv()
            gone[0] = pair_sum(2).astype(BF16)
            away(0, ahead).start()
        if d == 3:
            to_twin(1).wait_recv()
        if d == 0:
            to_twin(3).wait_recv()
            gone[2] = pair_sum(bwd).astype(BF16)
            away(2, behind).start()
    away(0, ahead).wait_recv()
    gone[1] = (pair_sum(fwd) + landed[0].astype(F32)).astype(BF16)
    away(1, ahead).start()
    to_twin(0).wait_recv()
    total = pair_sum(0)
    away(2, behind).wait_recv()
    total = total + landed[2].astype(F32)
    away(1, ahead).wait_recv()
    out_ref[...] = (total + landed[1].astype(F32)).astype(BF16)
    for d in order:
        to_twin(d).wait_send()
    for i in range(3):
        away(i, ahead).wait_send()


def output_part(nh, qeff, olocal, entry, gate, gain, weight):
    vm = pl.BlockSpec(memory_space=pltpu.VMEM)
    rows = qeff.shape[0] // nh
    width = weight.shape[1]
    chips = nh // 2
    return pl.pallas_call(
        functools.partial(output_kernel, nh),
        name="gated_projection",
        out_shape=jax.ShapeDtypeStruct((rows, width), BF16),
        in_specs=[vm] * 6,
        out_specs=vm,
        scratch_shapes=[
            pltpu.VMEM((2 * rows, weight.shape[0]), BF16),
            pltpu.VMEM((chips, rows, width), F32),
            pltpu.VMEM((chips, rows, width), BF16),
            pltpu.VMEM((chips, rows, width), BF16),
            pltpu.VMEM((3, rows, width), BF16),
            pltpu.VMEM((3, rows, width), BF16),
            pltpu.SemaphoreType.DMA((chips,)),
            pltpu.SemaphoreType.DMA((chips,)),
            pltpu.SemaphoreType.DMA((3,)),
            pltpu.SemaphoreType.DMA((3,)),
        ],
        compiler_params=pltpu.CompilerParams(
            collective_id=2, has_side_effects=True, vmem_limit_bytes=VMEM_LIMIT
        ),
    )(qeff, olocal, entry, gate, gain, weight)


def on_device(
    ns, nh, query_input, key_input, value_input, gate_input, write_strength, log_decay,
    filter_query, filter_key, filter_value, norm_gain, out_weight,
):
    small = jnp.concatenate([write_strength, log_decay], axis=1)
    q, k, v, wl = exchange(ns, nh, (query_input, key_input, value_input, small))
    own, qeff, olocal = local_terms(q, k, v, wl, filter_query, filter_key, filter_value)
    entry, gate = state_chain(ns, nh, NZ, own, gate_input)
    return output_part(nh, qeff, olocal, entry, gate, norm_gain.reshape(1, DV), out_weight)


def solution(mesh):
    placed = (
        P(("seq", "head"), None),
        P(("seq", "head"), None),
        P(("seq", "head"), None),
        P(("seq", "head"), None),
        P(("seq", "head"), None),
        P(("seq", "head"), None),
        P(None, "head"),
        P(None, "head"),
        P(None, "head"),
        P(),
        P("head", None),
    )
    return jax.shard_map(
        functools.partial(on_device, mesh.shape["seq"], mesh.shape["head"]),
        mesh=mesh,
        in_specs=placed,
        out_specs=P(("seq", "head"), None),
        check_vma=False,
    )
```

time: 189 us -> 123 us (0.65)
  Pallas kernels: 184 us -> 118 us
    pallas_call x1, Pallas kernels: 67 us -> 18.7 us  [local_terms(): pl.pallas_call(local_kernel, name='local_terms', out_shape=[jax.ShapeDtyp...]
    pallas_call x4 -> x3, Pallas kernels: 117 us -> 98.9 us  [the longest x1 52.8 us: state_chain(): pl.pallas_call(functools.partial(chain_kernel, ns, nh, nz), name='state_c...]
where the time goes in v2:
time: 123 us; the launch traced here: 122 us
  Pallas kernels  118 us (96%)
  local copies, waits for them, and re-layouts  3.25 us (3%)
    pallas_call x1, Pallas kernels, state_chain(): pl.pallas_call(functools.partial(chain_kernel, ns, nh, nz), name='state_c...  52.8 us
    pallas_call x1, Pallas kernels, output_part(): pl.pallas_call(functools.partial(output_kernel, nh), name='gated_projecti...  23.8 us
    pallas_call x1, Pallas kernels, exchange(): pl.pallas_call(functools.partial(exchange_kernel, ns, nh, VIA), name='tok...  22.4 us
    pallas_call x1, Pallas kernels, local_terms(): pl.pallas_call(local_kernel, name='local_terms', out_shape=[jax.ShapeDtyp...  18.7 us
    unnamed x3, local copies, waits for them, and re-layouts  3.25 us

profile of v2, /device:TPU:121, one launch (start us, length us, event | category | flops | bytes accessed | tf_op | source)
XLA Modules:
  0.0 121.6 jit_solution(15832072460930968045)
XLA Ops:
  0.0 0.8 copy.12
  0.8 0.8 copy.13
  1.6 0.7 pad_maximum_fusion.wl
  2.3 22.4 %token_exchange.1 = (bf16[528,256]{1,0:T(8,128)(2,1)}, bf16[528,256]{1,0:T(8,128)(2,1)}, bf16[528,512]{1,0:T(8,128)(2,1)}, bf16[512,64]{1,0:T(8,128)(2,1)}) custom-call(bf16[64,2048]{1,0:T(8,128)(2,1)} %q.1, bf16[64,2048]{1,0:T(8,128)(2,1)} %k.1, bf16[64,4096]{1,0:T(8,128)(2,1)} %v.1, bf16[64,64]{1,0:T(8,128)(2,1)} %pad_maximum_fusion.wl), custom_call_target="tpu_custom_call" | custom-call | tf_op jit(solution)/shard_map/token_exchange/pallas_call | solution.py:221
  24.7 18.7 %local_terms.1 = (f32[16,64,128]{2,1,0:T(8,128)}, f32[512,512]{1,0:T(8,128)}, f32[512,512]{1,0:T(8,128)}) custom-call(bf16[528,256]{1,0:T(8,128)(2,1)} %get-tuple-element.14.q_ref, bf16[528,256]{1,0:T(8,128)(2,1)} %get-tuple-element.15.k_ref, bf16[528,512]{1,0:T(8,128)(2,1)} %get-tuple-element.16.v_ref, bf16[512,64]{1,0:T(8,128)(2,1)} %get-tuple-element.17.wl_ref, ...), custom_call_target="tpu_custom_call" | custom-call | tf_op jit(solution)/shard_map/local_terms/pallas_call | solution.py:487
  43.4 52.8 %state_chain.1 = (f32[8,64,128]{2,1,0:T(8,128)}, bf16[512,512]{1,0:T(8,128)(2,1)}) custom-call(f32[16,64,128]{2,1,0:T(8,128)} %get-tuple-element.20.own_ref, bf16[64,4096]{1,0:T(8,128)(2,1)} %gate_in.1), custom_call_target="tpu_custom_call" | custom-call | tf_op jit(solution)/shard_map/state_chain/pallas_call | solution.py:777
  96.1 23.8 %gated_projection.1 = bf16[64,2048]{1,0:T(8,128)(2,1)} custom-call(f32[512,512]{1,0:T(8,128)} %get-tuple-element.18.qeff_ref, f32[512,512]{1,0:T(8,128)} %get-tuple-element.19.olocal_ref, f32[8,64,128]{2,1,0:T(8,128)} %get-tuple-element.21.entry_ref, bf16[512,512]{1,0:T(8,128)(2,1)} %get-tuple-element.22.gate_ref, f32[1,128]{1,0:T(1,128)} %bitcast.1, ...), custom_call_target="tpu_custom_call" | custom-call | tf_op jit(solution)/shard_map/gated_projection/pallas_call | solution.py:910
  119.9 1.7 %copy.15 = bf16[64,2048]{1,0:T(8,128)(2,1)} copy(bf16[64,2048]{1,0:T(8,128)(2,1)} %gated_projection.1) | data formatting | bytes 524288
